TPU v7x, 32 devices: a whole 2x2x4 slice. The times are simulated.
32 devices in a mesh: region: 4 (over y, x), tile: 8 (over z, core).
Axes of the slice: x: 2, y: 2, z: 4, core: 2. Of those that a mesh axis runs over, the one named last changes fastest.
Arguments:
- right_side: float32 [16, 32, 32, 256], P('region', 'tile'), may hold values from -20 to 20
- coords: float32 [16, 32, 2, 256], P('region', 'tile'), may hold values from 0 to 1
- pair_list: int32 [8, 16, 32], P(None, 'region', 'tile'), may hold values from 0 to 1, as said below
Outputs:
- solution: float32 [16, 32, 32, 256], P('region', 'tile')
- residual: float32 [16, 32, 32, 256], P('region', 'tile')
Inputs may be any that keep to these rules, and one draw needn't show every extreme that they name: pair_list[k + 4] at a block equals pair_list[k] at its neighbour in direction k + 4, for k < 4; a direction that leaves the grid of 16 x 32 blocks is 0.
All inputs are finite; a program needn't handle non-finite values.
Results may differ from a plain program's by a relative error of at most 0.0003.
Values sent between devices are 32-bit elements; how exact they have to be, the bound alone decides.
No kernel may reach another device: no remote copies, remote signals or barrier semaphores. Data moves between devices by JAX's collectives and lax.ppermute only.
A program may use at most 64 MiB of HBM per device.

v0:
```python
import jax
import jax.numpy as jnp
import numpy as np
from jax import lax
from jax.sharding import PartitionSpec as P

ITERS = 2


LENGTH_SCALE = 0.2
TAPER_RANGE = 0.5
NUGGET = 3.0
GROUP = 8
FORWARD_OFFSETS = ((0, 1), (1, 0), (1, 1), (1, -1))


def passed_along(x, axis, by):
    count = lax.axis_size(axis)
    pairs = [(i, i + by) for i in range(count) if 0 <= i + by < count]
    return lax.ppermute(x, axis, pairs)


def kernel_tile(own_pts, other_pts, shift_a, shift_b):
    gap_x = other_pts[..., 0, None, :] + shift_a - own_pts[..., 0, :, None]
    gap_y = other_pts[..., 1, None, :] + shift_b - own_pts[..., 1, :, None]
    distance = jnp.sqrt(gap_x * gap_x + gap_y * gap_y)
    scaled = jnp.minimum(distance / TAPER_RANGE, 1.0)
    tapered = (1.0 - scaled) ** 4 * (4.0 * scaled + 1.0)
    return jnp.exp(-distance / LENGTH_SCALE) * tapered


def item_tables(row_count, col_count, offsets, self_weight):
    position = np.arange(row_count * col_count)
    grid_rows = position // col_count
    grid_cols = position % col_count
    own_tab, other_tab, shift_x, shift_y, weight = ([], [], [], [], [])
    for shift_a, shift_b in ((0, 0),) + offsets:
        own_tab.append((grid_rows + 1) * (col_count + 2) + grid_cols + 1)
        other_tab.append((grid_rows + 1 + shift_a) * (col_count + 2) + grid_cols + 1 + shift_b)
        shift_x.append(np.full(grid_rows.shape, float(shift_a)))
        shift_y.append(np.full(grid_rows.shape, float(shift_b)))
        weight.append(
            np.full(grid_rows.shape, self_weight if shift_a == 0 and shift_b == 0 else 1.0)
        )
    int_table = np.stack([np.concatenate(own_tab), np.concatenate(other_tab)]).astype(np.int32)
    float_table = np.stack(
        [np.concatenate(shift_x), np.concatenate(shift_y), np.concatenate(weight)]
    ).astype(np.float32)
    return (int_table, float_table)


def apply_listed(extended, listed, int_table, float_table):
    slot_count = extended.shape[0] * extended.shape[1]
    rhs_count = extended.shape[2] - 2
    points = extended.shape[3]
    flattened = extended.reshape(slot_count, rhs_count + 2, points)
    count = jnp.sum(listed)
    ranking = jnp.argsort(1 - listed, stable=True)
    ranking = jnp.concatenate([ranking, jnp.zeros((GROUP,), jnp.int32)])
    catalog = jnp.arange(listed.shape[0], dtype=jnp.int32)
    int_lookup = jnp.asarray(int_table)
    float_lookup = jnp.asarray(float_table)

    def one_turn(turn_at, summed):
        chosen = lax.dynamic_slice_in_dim(ranking, turn_at * GROUP, GROUP)
        is_live = turn_at * GROUP + jnp.arange(GROUP, dtype=jnp.int32) < count
        onehot = chosen[:, None] == catalog[None, :]
        own_idx = jnp.sum(jnp.where(onehot, int_lookup[0][None, :], 0), axis=1)
        other_idx = jnp.sum(jnp.where(onehot, int_lookup[1][None, :], 0), axis=1)
        looked_up = jnp.sum(jnp.where(onehot[None], float_lookup[:, None, :], 0.0), axis=2)
        factor = jnp.where(is_live, looked_up[2], 0.0)
        own_rows = flattened[own_idx]
        other_rows = flattened[other_idx]
        cov_tile = (
            kernel_tile(
                own_rows[:, rhs_count:],
                other_rows[:, rhs_count:],
                looked_up[0][:, None, None],
                looked_up[1][:, None, None],
            )
            * factor[:, None, None]
        )
        to_own = jnp.einsum(
            "gpq,grq->grp", cov_tile, other_rows[:, :rhs_count], precision=lax.Precision.HIGHEST
        )
        summed = summed.at[own_idx].add(to_own)
        to_other = jnp.einsum(
            "gpq,grp->grq", cov_tile, own_rows[:, :rhs_count], precision=lax.Precision.HIGHEST
        )
        summed = summed.at[other_idx].add(to_other)
        return summed

    turn_count = (count + GROUP - 1) // GROUP
    zeros_init = jnp.zeros((slot_count, rhs_count, points), jnp.float32)
    summed = lax.fori_loop(0, turn_count, one_turn, zeros_init)
    return summed.reshape(extended.shape[0], extended.shape[1], rhs_count, points)


def operate(vector, coords, pair_list):
    row_count, col_count = (vector.shape[0], vector.shape[1])
    stacked = jnp.concatenate([vector, coords], axis=2)
    self_listed = jnp.ones((row_count * col_count,), jnp.int32)
    east_in = passed_along(stacked[:, 0], "tile", -1)
    west_in = passed_along(stacked[:, col_count - 1], "tile", 1)
    widened = jnp.concatenate([west_in[:, None], stacked, east_in[:, None]], axis=1)
    north_in = passed_along(widened[0], "region", -1)
    extended = jnp.concatenate([jnp.zeros_like(widened[:1]), widened, north_in[None]], axis=0)
    int_table, float_table = item_tables(row_count, col_count, FORWARD_OFFSETS, 0.5)
    listed = jnp.concatenate([self_listed, pair_list[:4].reshape(-1)])
    summed = apply_listed(extended, listed, int_table, float_table)
    east_back = passed_along(summed[:, col_count + 1], "tile", 1)
    west_back = passed_along(summed[:, 0], "tile", -1)
    summed = summed.at[:, 1].add(east_back).at[:, col_count].add(west_back)
    north_back = passed_along(summed[row_count + 1, 1 : col_count + 1], "region", 1)
    summed = summed.at[1, 1 : col_count + 1].add(north_back)
    return summed[1 : row_count + 1, 1 : col_count + 1] + NUGGET * vector


def inner_sum(left, right):
    return jnp.sum(left * right, axis=(0, 1, 3))


def per_rhs(values):
    return values[None, None, :, None]


def two_products(residual, image_field):
    return lax.psum(
        (inner_sum(residual, residual), inner_sum(residual, image_field)), ("region", "tile")
    )


def per_device(right_side, coords, pair_list):
    solution = jnp.zeros_like(right_side)
    residual = right_side
    image_field = operate(residual, coords, pair_list)
    norm_now, product = two_products(residual, image_field)
    step_len = norm_now / product
    direction = residual
    image_dir = image_field
    for iteration in range(ITERS):
        solution = solution + per_rhs(step_len) * direction
        residual = residual - per_rhs(step_len) * image_dir
        if iteration + 1 < ITERS:
            image_field = operate(residual, coords, pair_list)
            norm_next, product = two_products(residual, image_field)
            beta_val = norm_next / norm_now
            step_len = norm_next / (product - beta_val * norm_next / step_len)
            direction = residual + per_rhs(beta_val) * direction
            image_dir = image_field + per_rhs(beta_val) * image_dir
            norm_now = norm_next
    return (solution, residual)


def solution(mesh):
    placed = (
        P("region", "tile", None, None),
        P("region", "tile", None, None),
        P(None, "region", "tile"),
    )
    return jax.shard_map(
        per_device,
        mesh=mesh,
        in_specs=placed,
        out_specs=(P("region", "tile", None, None), P("region", "tile", None, None)),
        check_vma=False,
    )
```

profile of v0, /device:TPU:0, one launch (start us, length us, event | category | flops | bytes accessed | tf_op | source)
XLA Modules:
  0.0 449.2 jit_solution(1359898757321054193)
XLA Ops:
  0.6 1.2 multiply_reduce_fusion.3
  2.7 2.4 collective-permute-start
  5.1 1.3 collective-permute-start.1
  6.6 3.9 collective-permute-done.1
  10.6 1.3 collective-permute-start.2
  13.2 2.5 sort.19
  15.8 2.9 collective-permute-done.2
  19.3 48.9 %while.30 = (s32[]{:T(128)}, f32[36,32,256]{2,1,0:T(8,128)S(1)}, s32[]{:T(128)}, s32[88]{0:T(128)S(1)}, f32[36,34,256]{2,1,0:T(8,128)S(1)}, /*index=5*/s32[]{:T(...) while((s32[]{:T(128)}, f32[36,32,256]{2,1,0:T(8,128)S(1)}, ...), condition=%wide.region_10.11_spmd.clone.clone, body=%wide.region_4.10_spmd.sunk.clone.clone.sunk | while | flops 420623904 | bytes 4993907 | solution.py:95
  21.7 3.9 fusion.65
  25.6 4.1 fusion.64
  29.7 0.9 scatter_fusion
  30.6 0.9 scatter_fusion.1
  34.0 3.9 fusion.65
  37.8 4.1 fusion.64
  42.0 0.9 scatter_fusion
  46.2 3.9 fusion.65
  50.1 4.1 fusion.64
  54.2 0.9 scatter_fusion
  58.4 3.9 fusion.65
  62.3 4.1 fusion.64
  68.4 4.7 %collective-permute-start.3 = (f32[6,32,256]{2,1,0:T(8,128)S(1)}, f32[6,32,256]{2,1,0:T(8,128)S(1)}, u32[]{:S(2)}, u32[]{:S(2)}) collective-permute-start(f32[6,32,256]{2,1,0:T(8,128)S(1)} %slice_bitcast_fusion.7), channel_id=1, source_target_pairs={{0,1},{1,2},{2,3},{3,4},{4,5},{5,6},{6,7},{8,9},{9,10},{10,11},{11... | collective-permute-start | bytes 589832 | tf_op jit(solution)/shard_map/ppermute | solution.py:20
  73.2 1.3 collective-permute-start.4
  74.5 4.2 collective-permute-done.4
  78.8 4.3 collective-permute-start.5
  83.1 2.5 collective-permute-done.5
  85.9 115.8 %all-reduce.3 = (f32[32]{0:T(128)S(1)}, f32[32]{0:T(128)S(1)}) all-reduce(f32[32]{0:T(128)S(1)} %get-tuple-element.324, f32[32]{0:T(128)S(1)} %multiply_reduce_fusion.2), channel_id=1, replica_groups=mesh['region'=4,'tile'=8] {'region','tile'}, use_global_device_ids=true, to_apply=%region_1.0 | all-reduce | flops 64 | bytes 512 | tf_op jit(solution)/shard_map/psum | solution.py:128
  201.9 1.3 collective-permute-start.6
  203.2 1.3 collective-permute-start.7
  204.5 2.6 collective-permute-done.7
  207.2 1.3 collective-permute-start.8
  208.5 7.1 %collective-permute-done.8 = f32[6,34,256]{2,1,0:T(8,128)S(1)} collective-permute-done((f32[6,34,256]{2,1,0:T(8,128)S(1)}, f32[6,34,256]{2,1,0:T(8,128)S(1)}, u32[]{:S(2)}, u32[]{:S(2)}) %collective-permute-start.8) | collective-permute-done | bytes 208928 | tf_op jit(solution)/shard_map/ppermute | solution.py:20
  216.4 66.3 %while.31 = (s32[]{:T(128)}, f32[36,32,256]{2,1,0:T(8,128)S(1)}, s32[]{:T(128)}, s32[88]{0:T(128)S(1)}, f32[36,34,256]{2,1,0:T(8,128)S(1)}, /*index=5*/s32[]{:T(...) while((s32[]{:T(128)}, f32[36,32,256]{2,1,0:T(8,128)S(1)}, ...), condition=%wide.region_21.22_spmd.clone.clone, body=%wide.region_15.21_spmd.sunk.clone.clone.sunk | while | flops 420623904 | bytes 3946267 | solution.py:95
  218.1 1.3 gather_fusion.2
  219.4 0.9 fusion.69
  220.4 4.6 %fusion.71 = f32[8,32,256]{2,1,0:T(8,128)} fusion(f32[8]{0:T(128)S(1)} %compare_select_fusion.9, f32[8,256]{1,0:T(8,128)S(1)} %bitcast.178, f32[8,256]{1,0:T(8,128)S(1)} %bitcast.170, f32[8,256]{1,0:T(8,128)S(1)} %bitcast.182, f32[8,256]{1,0:T(8,128)S(1)} %bitcast.174, f32[8,34,256]{2,1,0:T(8,128)} %gather_fusion.2), kind=kOutput, calls=%fused_computation.43.clone.1 | convolution fusion | flops 210239488 | bytes 557088 | tf_op jit(solution)/shard_map/while/body/gpq,grp->grq/dot_general | solution.py:87
  225.0 4.4 fusion.70
  229.4 1.7 scatter_fusion.2
  231.1 1.7 scatter_fusion.3
  234.7 1.3 gather_fusion.2
  236.0 0.9 fusion.69
  237.0 4.6 %fusion.71 = f32[8,32,256]{2,1,0:T(8,128)} fusion(f32[8]{0:T(128)S(1)} %compare_select_fusion.9, f32[8,256]{1,0:T(8,128)S(1)} %bitcast.178, f32[8,256]{1,0:T(8,128)S(1)} %bitcast.170, f32[8,256]{1,0:T(8,128)S(1)} %bitcast.182, f32[8,256]{1,0:T(8,128)S(1)} %bitcast.174, f32[8,34,256]{2,1,0:T(8,128)} %gather_fusion.2), kind=kOutput, calls=%fused_computation.43.clone.1 | convolution fusion | flops 210239488 | bytes 557088 | tf_op jit(solution)/shard_map/while/body/gpq,grp->grq/dot_general | solution.py:87
  241.6 4.4 fusion.70
  246.0 1.7 scatter_fusion.2
  247.7 1.7 scatter_fusion.3
  251.3 1.3 gather_fusion.2
  252.6 0.9 fusion.69
  253.5 4.6 %fusion.71 = f32[8,32,256]{2,1,0:T(8,128)} fusion(f32[8]{0:T(128)S(1)} %compare_select_fusion.9, f32[8,256]{1,0:T(8,128)S(1)} %bitcast.178, f32[8,256]{1,0:T(8,128)S(1)} %bitcast.170, f32[8,256]{1,0:T(8,128)S(1)} %bitcast.182, f32[8,256]{1,0:T(8,128)S(1)} %bitcast.174, f32[8,34,256]{2,1,0:T(8,128)} %gather_fusion.2), kind=kOutput, calls=%fused_computation.43.clone.1 | convolution fusion | flops 210239488 | bytes 557088 | tf_op jit(solution)/shard_map/while/body/gpq,grp->grq/dot_general | solution.py:87
  258.2 4.4 fusion.70
  262.6 1.7 scatter_fusion.2
  264.3 1.7 scatter_fusion.3
  267.9 1.3 gather_fusion.2
  269.2 0.9 fusion.69
  270.1 4.6 %fusion.71 = f32[8,32,256]{2,1,0:T(8,128)} fusion(f32[8]{0:T(128)S(1)} %compare_select_fusion.9, f32[8,256]{1,0:T(8,128)S(1)} %bitcast.178, f32[8,256]{1,0:T(8,128)S(1)} %bitcast.170, f32[8,256]{1,0:T(8,128)S(1)} %bitcast.182, f32[8,256]{1,0:T(8,128)S(1)} %bitcast.174, f32[8,34,256]{2,1,0:T(8,128)} %gather_fusion.2), kind=kOutput, calls=%fused_computation.43.clone.1 | convolution fusion | flops 210239488 | bytes 557088 | tf_op jit(solution)/shard_map/while/body/gpq,grp->grq/dot_general | solution.py:87
  274.8 4.4 fusion.70
  279.2 1.7 scatter_fusion.2
  280.9 1.7 scatter_fusion.3
  282.7 4.9 %collective-permute-start.9 = (f32[6,32,256]{2,1,0:T(8,128)S(1)}, f32[6,32,256]{2,1,0:T(8,128)S(1)}, u32[]{:S(2)}, u32[]{:S(2)}) collective-permute-start(f32[6,32,256]{2,1,0:T(8,128)S(1)} %slice_bitcast_fusion.5), channel_id=1, source_target_pairs={{0,1},{1,2},{2,3},{3,4},{4,5},{5,6},{6,7},{8,9},{9,10},{10,11},{11... | collective-permute-start | bytes 589832 | tf_op jit(solution)/shard_map/ppermute | solution.py:20
  287.6 1.0 collective-permute-done.9
  288.7 1.3 collective-permute-start.10
  290.0 5.5 %collective-permute-done.10 = f32[6,32,256]{2,1,0:T(8,128)S(1)} collective-permute-done((f32[6,32,256]{2,1,0:T(8,128)S(1)}, f32[6,32,256]{2,1,0:T(8,128)S(1)}, u32[]{:S(2)}, u32[]{:S(2)}) %collective-permute-start.10) | collective-permute-done | bytes 196640 | tf_op jit(solution)/shard_map/ppermute | solution.py:20
  295.7 5.2 %collective-permute-start.11 = (f32[4,32,256]{2,1,0:T(8,128)S(1)}, f32[4,32,256]{2,1,0:T(8,128)S(1)}, u32[]{:S(2)}, u32[]{:S(2)}) collective-permute-start(f32[4,32,256]{2,1,0:T(8,128)S(1)} %slice_bitcast_fusion.10), channel_id=1, source_target_pairs={{0,8},{8,16},{16,24},{1,9},{9,17},{17,25},{2,10},{10,18},{18,26},{... | collective-permute-start | bytes 393224 | tf_op jit(solution)/shard_map/ppermute | solution.py:20
  301.0 2.4 collective-permute-done.11
  303.7 142.4 %all-reduce.2 = (f32[32]{0:T(128)S(1)}, f32[32]{0:T(128)S(1)}) all-reduce(f32[32]{0:T(128)S(1)} %get-tuple-element.269, f32[32]{0:T(128)S(1)} %get-tuple-element.268), channel_id=1, replica_groups=mesh['region'=4,'tile'=8] {'region','tile'}, use_global_device_ids=true, to_apply=%region_14.15 | all-reduce | flops 64 | bytes 512 | tf_op jit(solution)/shard_map/psum | solution.py:128
  446.1 1.4 multiply_subtract_fusion
  (216 shorter events, 25.8 us)
Async XLA Ops:
  0.6 5.8 %copy-start.8 = (s32[8,4,4]{0,2,1:T(4,128)S(1)}, s32[8,4,4]{0,2,1:T(4,128)}, u32[]{:S(2)}) copy-start(s32[8,4,4]{0,2,1:T(4,128)} %param.25) | copy-start | bytes 1540
  2.7 3.9 collective-permute-start
  5.1 5.5 %collective-permute-start.1 = (f32[4,34,256]{2,1,0:T(8,128)S(1)}, f32[4,34,256]{2,1,0:T(8,128)S(1)}, u32[]{:S(2)}, u32[]{:S(2)}) collective-permute-start(f32[4,34,256]{2,1,0:T(8,128)S(1)} %get-tuple-element.321), channel_id=1, source_target_pairs={{1,0},{2,1},{3,2},{4,3},{5,4},{6,5},{7,6},{9,8},{10,9},{11,10},{12... | collective-permute-start | bytes 417800 | tf_op jit(solution)/shard_map/ppermute | solution.py:20
  10.6 8.1 %collective-permute-start.2 = (f32[6,34,256]{2,1,0:T(8,128)S(1)}, f32[6,34,256]{2,1,0:T(8,128)S(1)}, u32[]{:S(2)}, u32[]{:S(2)}) collective-permute-start(f32[6,34,256]{2,1,0:T(8,128)S(1)} %fusion.33), channel_id=1, source_target_pairs={{8,0},{16,8},{24,16},{9,1},{17,9},{25,17},{10,2},{18,10},{26,18},{... | collective-permute-start | bytes 626696 | tf_op jit(solution)/shard_map/ppermute | solution.py:20
  18.7 0.7 copy-start.5
  18.7 0.7 copy-start.6
  18.7 0.7 copy-start.7
  25.6 5.0 %copy-start.3 = (f32[8,32,256]{2,1,0:T(8,128)S(1)}, f32[8,32,256]{2,1,0:T(8,128)}, u32[]{:S(2)}) copy-start(f32[8,32,256]{2,1,0:T(8,128)} %fusion.65) | copy-start | bytes 786436 | tf_op jit(solution)/shard_map/while
  37.8 5.0 %copy-start.3 = (f32[8,32,256]{2,1,0:T(8,128)S(1)}, f32[8,32,256]{2,1,0:T(8,128)}, u32[]{:S(2)}) copy-start(f32[8,32,256]{2,1,0:T(8,128)} %fusion.65) | copy-start | bytes 786436 | tf_op jit(solution)/shard_map/while
  50.1 5.0 %copy-start.3 = (f32[8,32,256]{2,1,0:T(8,128)S(1)}, f32[8,32,256]{2,1,0:T(8,128)}, u32[]{:S(2)}) copy-start(f32[8,32,256]{2,1,0:T(8,128)} %fusion.65) | copy-start | bytes 786436 | tf_op jit(solution)/shard_map/while
  62.3 5.0 %copy-start.3 = (f32[8,32,256]{2,1,0:T(8,128)S(1)}, f32[8,32,256]{2,1,0:T(8,128)}, u32[]{:S(2)}) copy-start(f32[8,32,256]{2,1,0:T(8,128)} %fusion.65) | copy-start | bytes 786436 | tf_op jit(solution)/shard_map/while
  68.2 4.9 %copy-start.13 = (s32[88]{0:T(128)}, s32[88]{0:T(128)S(1)}, u32[]{:S(2)}) copy-start(s32[88]{0:T(128)S(1)} %get-tuple-element.549) | copy-start | bytes 1060
  68.4 17.3 %copy-start.1 = (f32[4,4,32,256]{3,2,1,0:T(8,128)S(1)}, f32[4,4,32,256]{3,2,1,0:T(8,128)}, u32[]{:S(2)}) copy-start(f32[4,4,32,256]{3,2,1,0:T(8,128)} %param.23) | copy-start | bytes 1572868
  68.4 6.1 %collective-permute-start.3 = (f32[6,32,256]{2,1,0:T(8,128)S(1)}, f32[6,32,256]{2,1,0:T(8,128)S(1)}, u32[]{:S(2)}, u32[]{:S(2)}) collective-permute-start(f32[6,32,256]{2,1,0:T(8,128)S(1)} %slice_bitcast_fusion.7), channel_id=1, source_target_pairs={{0,1},{1,2},{2,3},{3,4},{4,5},{5,6},{6,7},{8,9},{9,10},{10,11},{11... | collective-permute-start | bytes 589832 | tf_op jit(solution)/shard_map/ppermute | solution.py:20
  73.2 5.6 %collective-permute-start.4 = (f32[6,32,256]{2,1,0:T(8,128)S(1)}, f32[6,32,256]{2,1,0:T(8,128)S(1)}, u32[]{:S(2)}, u32[]{:S(2)}) collective-permute-start(f32[6,32,256]{2,1,0:T(8,128)S(1)} %slice_bitcast_fusion.6), channel_id=1, source_target_pairs={{1,0},{2,1},{3,2},{4,3},{5,4},{6,5},{7,6},{9,8},{10,9},{11,10},{12... | collective-permute-start | bytes 589832 | tf_op jit(solution)/shard_map/ppermute | solution.py:20
  78.8 123.1 %copy-start.4 = (f32[4,4,2,256]{3,2,1,0:T(2,128)S(1)}, f32[4,4,2,256]{3,2,1,0:T(2,128)}, u32[]{:S(2)}) copy-start(f32[4,4,2,256]{3,2,1,0:T(2,128)} %param.24) | copy-start | bytes 98308
  78.8 6.8 %collective-permute-start.5 = (f32[4,32,256]{2,1,0:T(8,128)S(1)}, f32[4,32,256]{2,1,0:T(8,128)S(1)}, u32[]{:S(2)}, u32[]{:S(2)}) collective-permute-start(f32[4,32,256]{2,1,0:T(8,128)S(1)} %slice_bitcast_fusion.12), channel_id=1, source_target_pairs={{0,8},{8,16},{16,24},{1,9},{9,17},{17,25},{2,10},{10,18},{18,26},{... | collective-permute-start | bytes 393224 | tf_op jit(solution)/shard_map/ppermute | solution.py:20
  85.7 116.2 %copy-start = (f32[6,6,32,256]{3,2,0,1:T(8,128)}, f32[6,6,32,256]{3,2,0,1:T(8,128)S(1)}, u32[]{:S(2)}) copy-start(f32[6,6,32,256]{3,2,0,1:T(8,128)S(1)} %fusion.41) | copy-start | bytes 3538948
  201.7 5.5 %copy-start.9 = (f32[32]{0:T(128)}, f32[32]{0:T(128)S(1)}, u32[]{:S(2)}) copy-start(f32[32]{0:T(128)S(1)} %get-tuple-element.296) | copy-start | bytes 388
  201.7 5.5 %copy-start.11 = (f32[32]{0:T(128)}, f32[32]{0:T(128)S(1)}, u32[]{:S(2)}) copy-start(f32[32]{0:T(128)S(1)} %get-tuple-element.297) | copy-start | bytes 388
  201.9 2.6 collective-permute-start.6
  203.2 4.0 collective-permute-start.7
  207.2 8.4 %collective-permute-start.8 = (f32[6,34,256]{2,1,0:T(8,128)S(1)}, f32[6,34,256]{2,1,0:T(8,128)S(1)}, u32[]{:S(2)}, u32[]{:S(2)}) collective-permute-start(f32[6,34,256]{2,1,0:T(8,128)S(1)} %fusion.32), channel_id=1, source_target_pairs={{8,0},{16,8},{24,16},{9,1},{17,9},{25,17},{10,2},{18,10},{26,18},{... | collective-permute-start | bytes 626696 | tf_op jit(solution)/shard_map/ppermute | solution.py:20
  215.8 0.6 copy-start.14
  229.4 3.5 copy-start.15
  246.0 3.5 copy-start.15
  262.6 3.5 copy-start.15
  279.2 3.5 copy-start.15
  282.7 5.9 %collective-permute-start.9 = (f32[6,32,256]{2,1,0:T(8,128)S(1)}, f32[6,32,256]{2,1,0:T(8,128)S(1)}, u32[]{:S(2)}, u32[]{:S(2)}) collective-permute-start(f32[6,32,256]{2,1,0:T(8,128)S(1)} %slice_bitcast_fusion.5), channel_id=1, source_target_pairs={{0,1},{1,2},{2,3},{3,4},{4,5},{5,6},{6,7},{8,9},{9,10},{10,11},{11... | collective-permute-start | bytes 589832 | tf_op jit(solution)/shard_map/ppermute | solution.py:20
  288.7 6.8 %collective-permute-start.10 = (f32[6,32,256]{2,1,0:T(8,128)S(1)}, f32[6,32,256]{2,1,0:T(8,128)S(1)}, u32[]{:S(2)}, u32[]{:S(2)}) collective-permute-start(f32[6,32,256]{2,1,0:T(8,128)S(1)} %get-tuple-element.316), channel_id=1, source_target_pairs={{1,0},{2,1},{3,2},{4,3},{5,4},{6,5},{7,6},{9,8},{10,9},{11,10},{12... | collective-permute-start | bytes 589832 | tf_op jit(solution)/shard_map/ppermute | solution.py:20
  295.6 150.4 %copy-start.10 = (f32[32]{0:T(128)S(1)}, f32[32]{0:T(128)}, u32[]{:S(2)}) copy-start(f32[32]{0:T(128)} %copy-done.9) | copy-start | bytes 388
  295.7 150.4 %copy-start.12 = (f32[32]{0:T(128)S(1)}, f32[32]{0:T(128)}, u32[]{:S(2)}) copy-start(f32[32]{0:T(128)} %copy-done.11) | copy-start | bytes 388
  295.7 150.4 %copy-start.2 = (f32[4,4,32,256]{3,2,1,0:T(8,128)S(1)}, f32[4,4,32,256]{3,2,1,0:T(8,128)}, u32[]{:S(2)}) copy-start(f32[4,4,32,256]{3,2,1,0:T(8,128)} %param.23) | copy-start | bytes 1572868
  295.7 7.7 %collective-permute-start.11 = (f32[4,32,256]{2,1,0:T(8,128)S(1)}, f32[4,32,256]{2,1,0:T(8,128)S(1)}, u32[]{:S(2)}, u32[]{:S(2)}) collective-permute-start(f32[4,32,256]{2,1,0:T(8,128)S(1)} %slice_bitcast_fusion.10), channel_id=1, source_target_pairs={{0,8},{8,16},{16,24},{1,9},{9,17},{17,25},{2,10},{10,18},{18,26},{... | collective-permute-start | bytes 393224 | tf_op jit(solution)/shard_map/ppermute | solution.py:20
where the time goes:
time: 451 us; the launch traced here: 449 us
  blocking collectives  258 us (57%)
  matrix products  68.1 us (15%)
  other arithmetic  36.6 us (8%)
  waiting for transfers between devices  32.2 us (7%)
  starting transfers between devices  30.6 us (7%)
  local copies, waits for them, and re-layouts  20.7 us (5%)
    psum x2, blocking collectives, two_products(): lax.psum((inner_sum(residual, residual), inner_sum(residual, image_field)...  258 us
    dot_general x8, matrix products, one_turn(): jnp.einsum('gpq,grp->grq', cov_tile, own_rows[:, :rhs_count], precision=l...  34.1 us
    dot_general x8, matrix products, one_turn(): jnp.einsum('gpq,grq->grp', cov_tile, other_rows[:, :rhs_count], precision...  34.1 us
    ppermute x12, waiting for transfers between devices, passed_along(): return lax.ppermute(x, axis, pairs)  32.2 us
    ppermute x12, starting transfers between devices, passed_along(): return lax.ppermute(x, axis, pairs)  30.6 us
    scatter-add x8, other arithmetic, one_turn(): summed = summed.at[other_idx].add(to_other)  10.5 us
    scatter-add x8, other arithmetic, one_turn(): summed = summed.at[own_idx].add(to_own)  10.5 us
  transfers between devices with their start and end apart: 12, of which 9 were waited for; matrix products, arithmetic and copies ran while one was open for 1% of the time, Pallas kernels for 0%

commit v1 on v0

v1 whole, which is shorter than its diff:
```python
import functools

import jax
import jax.numpy as jnp
from jax import lax
from jax.experimental import pallas as pl
from jax.experimental.pallas import tpu as pltpu
from jax.sharding import PartitionSpec as P

LENGTH_SCALE = 0.2
TAPER_RANGE = 0.5
NUGGET = 3.0
OFFSETS = ((0, 1), (1, 0), (1, 1), (1, -1), (0, -1), (-1, 0), (-1, -1), (-1, 1))
FACTOR = 4.0**0.2
UNIT = FACTOR / TAPER_RANGE
DECAY = -1.4426950408889634 / (LENGTH_SCALE * UNIT)
STRIP = 64
VMEM_LIMIT = 48 * 1024 * 1024


def dot_nn(a, b):
    return lax.dot_general(a, b, (((1,), (0,)), ((), ())), preferred_element_type=jnp.float32)


def dot_nt(a, b):
    return lax.dot_general(a, b, (((1,), (1,)), ((), ())), preferred_element_type=jnp.float32)


def split_hi_lo(values):
    hi = values.astype(jnp.bfloat16)
    lo = (values - hi.astype(jnp.float32)).astype(jnp.bfloat16)
    return hi, lo


def across_lanes(row, lanes):
    return jnp.transpose(jnp.broadcast_to(row, (lanes, row.shape[1])))


def make_tile(tile_ref, spread_ref, other, points_ref, own, shift_a, shift_b):
    points = tile_ref.shape[1]
    lanes = spread_ref.shape[3]
    own_x = points_ref[own, 0:1] - shift_a
    own_y = points_ref[own, 1:2] - shift_b
    for start in range(0, points, STRIP):
        rows = slice(start, start + STRIP)
        for left in range(0, points, lanes):
            cols = slice(left, left + lanes)
            gap_x = spread_ref[other, 0, rows] - own_x[:, cols]
            gap_y = spread_ref[other, 1, rows] - own_y[:, cols]
            square = jnp.maximum(gap_x * gap_x + gap_y * gap_y, 1e-30)
            dist = square * lax.rsqrt(square)
            rest = jnp.maximum(FACTOR - dist, 0.0)
            rest2 = rest * rest
            cov = (jnp.exp2(dist * DECAY) * (rest2 * rest2)) * (1.25 * FACTOR - rest)
            hi, lo = split_hi_lo(cov)
            tile_ref[0, rows, cols] = hi
            tile_ref[1, rows, cols] = lo


def product(dot, parts_ref, at, tile_ref):
    rhs = parts_ref.shape[1] // 2
    both = dot(parts_ref[at], tile_ref[0])
    cross = dot(parts_ref[at, 0:rhs], tile_ref[1])
    return both[:rhs] + both[rhs:] + cross


def store_parts(parts_ref, at, values):
    rhs = values.shape[0]
    hi, lo = split_hi_lo(values)
    parts_ref[at, 0:rhs] = hi
    parts_ref[at, rhs : 2 * rhs] = lo


def run_items(items_ref, count, tile_a, tile_b, make, use):
    tile_b[...] = jnp.zeros_like(tile_b)

    def one_turn(turn, carry):
        use(tile_b, items_ref[2 * turn])
        make(tile_a, items_ref[2 * turn + 1])
        use(tile_a, items_ref[2 * turn + 1])
        make(tile_b, items_ref[2 * turn + 2])
        return carry

    turns = (count + 1) // 2
    lax.fori_loop(0, turns, one_turn, 0)
    use(tile_b, items_ref[2 * turns])


def item_code(own, other, shift_a, shift_b):
    return own + 64 * other + 4096 * (shift_a + 1) + 16384 * (shift_b + 1)


NO_ITEM = item_code(0, 0, 2, 2)


def item_fields(code):
    own = lax.rem(code, 64)
    other = lax.rem(code // 64, 64)
    shift_a = (lax.rem(code // 4096, 4) - 1).astype(jnp.float32) * UNIT
    shift_b = (code // 16384 - 1).astype(jnp.float32) * UNIT
    return own, other, shift_a, shift_b


def list_items(items_ref, candidates, pair_ref):
    items_ref[0] = NO_ITEM
    count = jnp.int32(0)
    for k, own, code in candidates:
        items_ref[count + 1] = code
        count = count + jnp.where(pair_ref[k, own] > 0, 1, 0)
    items_ref[count + 1] = NO_ITEM
    items_ref[count + 2] = NO_ITEM
    return count


def self_kernel(v_ref, c_ref, out_ref, parts_ref, points_ref, spread_ref, tile_a, tile_b):
    blocks = v_ref.shape[0]
    lanes = spread_ref.shape[3]

    def prepare(at, carry):
        store_parts(parts_ref, at, v_ref[at])
        out_ref[at] = NUGGET * v_ref[at]
        points_ref[at] = c_ref[at] * UNIT
        for axis in range(2):
            spread_ref[at, axis] = across_lanes(points_ref[at, axis : axis + 1], lanes)
        return carry

    lax.fori_loop(0, blocks, prepare, 0)
    tile_b[...] = jnp.zeros_like(tile_b)

    def use(tile_ref, at):
        out_ref[at] += product(dot_nn, parts_ref, at, tile_ref)

    def one_turn(turn, carry):
        first = 2 * turn
        use(tile_b, jnp.maximum(first - 1, 0))
        make_tile(tile_a, spread_ref, first, points_ref, first, 0.0, 0.0)
        use(tile_a, first)
        make_tile(tile_b, spread_ref, first + 1, points_ref, first + 1, 0.0, 0.0)
        return carry

    lax.fori_loop(0, blocks // 2, one_turn, 0)
    use(tile_b, blocks - 1)


def inner_kernel(
    shape, pair_ref, v_ref, c_ref, sum_ref, out_ref, items_ref, parts_ref, points_ref, spread_ref, tile_a, tile_b
):
    rows, cols = shape
    lanes = spread_ref.shape[3]

    def prepare(at, carry):
        store_parts(parts_ref, at, v_ref[at])
        out_ref[at] = sum_ref[at]
        points_ref[at] = c_ref[at] * UNIT
        for axis in range(2):
            spread_ref[at, axis] = across_lanes(points_ref[at, axis : axis + 1], lanes)
        return carry

    lax.fori_loop(0, rows * cols, prepare, 0)
    candidates = []
    for k in range(4):
        shift_a, shift_b = OFFSETS[k]
        for a in range(rows):
            for b in range(cols):
                if 0 <= a + shift_a < rows and 0 <= b + shift_b < cols:
                    own = a * cols + b
                    other = own + shift_a * cols + shift_b
                    candidates.append((k, own, item_code(own, other, shift_a, shift_b)))
    count = list_items(items_ref, candidates, pair_ref)

    def make(tile_ref, code):
        own, other, shift_a, shift_b = item_fields(code)
        make_tile(tile_ref, spread_ref, other, points_ref, own, shift_a, shift_b)

    def use(tile_ref, code):
        own, other, _, _ = item_fields(code)
        out_ref[own] += product(dot_nn, parts_ref, other, tile_ref)
        out_ref[other] += product(dot_nt, parts_ref, own, tile_ref)

    run_items(items_ref, count, tile_a, tile_b, make, use)


def cross_kernel(shape, last, *refs):
    rows, cols = shape
    pair_ref, c_ref, sum_ref = refs[:3]
    halo_v, halo_c = refs[3:7], refs[7:11]
    refs = refs[11:]
    if last:
        v0_ref, v1_ref = refs[:2]
        out_ref, moments_ref = refs[2:4]
        refs = refs[4:]
    else:
        out_ref = refs[0]
        refs = refs[1:]
    items_ref, parts_ref, points_ref, spread_ref, tile_a, tile_b = refs
    lanes = spread_ref.shape[3]
    rhs = out_ref.shape[1]

    def prepare(at, carry):
        out_ref[at] = sum_ref[at]
        points_ref[at] = c_ref[at] * UNIT
        return carry

    lax.fori_loop(0, rows * cols, prepare, 0)

    slots = {}
    for side, length in enumerate((rows, rows, cols + 2, cols + 2)):
        for at in range(length):
            slot = len(slots)
            place = ((at, -1), (at, cols), (-1, at - 1), (rows, at - 1))[side]
            slots[place] = slot
    candidates = []
    for k in range(8):
        shift_a, shift_b = OFFSETS[k]
        for a in range(rows):
            for b in range(cols):
                place = (a + shift_a, b + shift_b)
                if place in slots:
                    own = a * cols + b
                    candidates.append((k, own, item_code(own, slots[place], shift_a, shift_b)))
    count = list_items(items_ref, candidates, pair_ref)

    start = 0
    for side, length in enumerate((rows, rows, cols + 2, cols + 2)):

        def take(at, carry, side=side, start=start):
            store_parts(parts_ref, start + at, halo_v[side][at, 0:rhs])
            for axis in range(2):
                row = halo_c[side][at, rhs + axis : rhs + axis + 1] * UNIT
                spread_ref[start + at, axis] = across_lanes(row, lanes)
            return carry

        lax.fori_loop(0, length, take, 0)
        start += length

    def make(tile_ref, code):
        own, other, shift_a, shift_b = item_fields(code)
        make_tile(tile_ref, spread_ref, other, points_ref, own, shift_a, shift_b)

    def use(tile_ref, code):
        own, other, _, _ = item_fields(code)
        out_ref[own] += product(dot_nn, parts_ref, other, tile_ref)

    run_items(items_ref, count, tile_a, tile_b, make, use)
    if last:
        zero = jnp.zeros(out_ref.shape[1:], jnp.float32)

        def gather(at, sums):
            w0, w1, w2 = v0_ref[at], v1_ref[at], out_ref[at]
            terms = (w0 * w0, w0 * w1, w1 * w1, w1 * w2)
            return tuple(s + t for s, t in zip(sums, terms))

        sums = lax.fori_loop(0, rows * cols, gather, (zero,) * 4)
        folded = [sum(s[:, left : left + lanes] for left in range(0, s.shape[1], lanes)) for s in sums]
        stacked = jnp.concatenate(folded, axis=0)
        line = jnp.sum(jnp.transpose(stacked), axis=0, keepdims=True)
        moments_ref[...] = jnp.broadcast_to(line[None], moments_ref.shape)


def final_kernel(moments_ref, v0_ref, v1_ref, v2_ref, solution_ref, residual_ref):
    rhs, points = v0_ref.shape[1:]
    line = moments_ref[0]
    for at in range(1, moments_ref.shape[0]):
        line = line + moments_ref[at]
    table = across_lanes(line, line.shape[1])
    m00, m01, m11, m12 = (table[k * rhs : (k + 1) * rhs] for k in range(4))
    a = m00 / m01
    norm = m00 - 2.0 * a * m01 + a * a * m11
    grow = 1.0 + norm / m00
    step = norm / (grow * (grow * m01 - 2.0 * a * m11) + a * a * m12)
    first = jnp.concatenate([a + step * grow] * (points // line.shape[1]), axis=1)
    second = jnp.concatenate([step * a] * (points // line.shape[1]), axis=1)

    def one(at, carry):
        w0, w1, w2 = v0_ref[at], v1_ref[at], v2_ref[at]
        solution_ref[at] = first * w0 - second * w1
        residual_ref[at] = w0 - first * w1 + second * w2
        return carry

    lax.fori_loop(0, v0_ref.shape[0], one, 0)


def passed_along(x, axis, by):
    count = lax.axis_size(axis)
    pairs = [(i, i + by) for i in range(count) if 0 <= i + by < count]
    return lax.ppermute(x, axis, pairs)


def per_device(right_side, coords, pair_list):
    rows, cols, rhs, points = right_side.shape
    blocks = rows * cols
    devices = lax.axis_size("region") * lax.axis_size("tile")
    lanes = 128
    f32 = jnp.float32
    field = jax.ShapeDtypeStruct((blocks, rhs, points), f32)
    pairs = pair_list.reshape(8, blocks)
    own_points = coords.reshape(blocks, 2, points)
    vmem = pl.BlockSpec(memory_space=pltpu.VMEM)
    smem = pl.BlockSpec(memory_space=pltpu.SMEM)
    params = pltpu.CompilerParams(vmem_limit_bytes=VMEM_LIMIT)
    tile = pltpu.VMEM((2, points, points), jnp.bfloat16)
    halo = 2 * rows + 2 * (cols + 2)

    def scratch(others, listed):
        shapes = [
            pltpu.VMEM((others, 2 * rhs, points), jnp.bfloat16),
            pltpu.VMEM((blocks, 2, points), f32),
            pltpu.VMEM((others, 2, points, lanes), f32),
            tile,
            tile,
        ]
        return ([pltpu.SMEM((listed + 3,), jnp.int32)] if listed else []) + shapes

    def cost(tiles):
        return pl.CostEstimate(
            flops=tiles * 6 * rhs * points * points,
            transcendentals=tiles * 2 * points * points,
            bytes_accessed=4 * blocks * rhs * points * 4,
        )

    def self_part(v):
        return pl.pallas_call(
            self_kernel, out_shape=field, in_specs=[vmem] * 2, out_specs=vmem,
            scratch_shapes=scratch(blocks, 0), compiler_params=params, cost_estimate=cost(blocks), name="own_blocks",
        )(v, own_points)

    def inner_part(v, summed):
        return pl.pallas_call(
            functools.partial(inner_kernel, (rows, cols)), out_shape=field, in_specs=[smem] + [vmem] * 3,
            out_specs=vmem, scratch_shapes=scratch(blocks, 4 * blocks), compiler_params=params,
            cost_estimate=cost(3 * blocks), name="inner_pairs",
        )(pairs, v, own_points, summed)

    def cross_part(summed, halo_v, halo_c, others=None):
        last = others is not None
        out_shape = (field, jax.ShapeDtypeStruct((devices, 1, 4 * rhs), f32)) if last else field
        return pl.pallas_call(
            functools.partial(cross_kernel, (rows, cols), last), out_shape=out_shape,
            in_specs=[smem] + [vmem] * (12 if last else 10), out_specs=(vmem, vmem) if last else vmem,
            scratch_shapes=scratch(halo, 8 * blocks), compiler_params=params,
            cost_estimate=cost(2 * blocks), name="cross_pairs",
        )(pairs, own_points, summed, *halo_v, *halo_c, *(others or ()))

    def apply(field_v, packed, halo_c, others=None):
        prev_col = passed_along(packed[:, cols - 1], "tile", 1)
        next_col = passed_along(packed[:, 0], "tile", -1)
        summed = self_part(field_v)
        top = jnp.concatenate([prev_col[:1], packed[0], next_col[:1]], axis=0)
        bottom = jnp.concatenate([prev_col[rows - 1 :], packed[rows - 1], next_col[rows - 1 :]], axis=0)
        prev_row = passed_along(bottom, "region", 1)
        next_row = passed_along(top, "region", -1)
        summed = inner_part(field_v, summed)
        halo_v = (prev_col, next_col, prev_row, next_row)
        return cross_part(summed, halo_v, halo_c or halo_v, others), halo_v

    w0 = right_side.reshape(blocks, rhs, points)
    w1, halo_c = apply(w0, jnp.concatenate([right_side, coords], axis=2), None)
    (w2, moments), _ = apply(w1, w1.reshape(right_side.shape), halo_c, (w0, w1))
    moments = lax.all_to_all(moments, ("region", "tile"), 0, 0)
    solution, residual = pl.pallas_call(
        final_kernel, out_shape=(field, field), in_specs=[vmem] * 4, out_specs=(vmem, vmem),
        compiler_params=params, name="final_update",
    )(moments, w0, w1, w2)
    return solution.reshape(right_side.shape), residual.reshape(right_side.shape)


def solution(mesh):
    placed = (
        P("region", "tile", None, None),
        P("region", "tile", None, None),
        P(None, "region", "tile"),
    )
    return jax.shard_map(
        per_device,
        mesh=mesh,
        in_specs=placed,
        out_specs=(P("region", "tile", None, None), P("region", "tile", None, None)),
        check_vma=False,
    )
```

time: 451 us -> 119 us (0.26)
  blocking collectives: 258 us -> 36.6 us
  matrix products: 68.1 us -> 0 us
  Pallas kernels: 0 us -> 36.8 us
  other arithmetic: 36.6 us -> 0.08 us
  waiting for transfers between devices: 32.2 us -> 1.87 us
  local copies, waits for them, and re-layouts: 20.7 us -> 1.3 us
  starting transfers between devices: 30.6 us -> 39.5 us
    psum x2 -> x0, blocking collectives: 258 us -> none  [two_products(): lax.psum((inner_sum(residual, residual), inner_sum(residual, image_field)...]
    dot_general x16 -> x0, matrix products: 68.1 us -> none  [the longest x8 34.1 us: one_turn(): jnp.einsum('gpq,grp->grq', cov_tile, own_rows[:, :rhs_count], precision=l...]
    pallas_call x0 -> x7, Pallas kernels: none -> 36.8 us  [the longest x2 13.7 us: self_part(): pl.pallas_call(self_kernel, out_shape=field, in_specs=[vmem] * 2, out_spe...]
    all_to_all x0 -> x1, blocking collectives: none -> 36.6 us  [per_device(): moments = lax.all_to_all(moments, ('region', 'tile'), 0, 0)]
    ppermute x12 -> x8, waiting for transfers between devices: 32.2 us -> 1.87 us  [passed_along(): return lax.ppermute(x, axis, pairs)]
    scatter-add x21 -> x0, other arithmetic: 21.3 us -> none  [the longest x8 10.5 us: one_turn(): summed = summed.at[other_idx].add(to_other)]
    gather x16 -> x0, local copies, waits for them, and re-layouts: 12 us -> none  [the longest x8 7.45 us: one_turn(): own_rows = flattened[own_idx]]
    ppermute x12 -> x8, starting transfers between devices: 30.6 us -> 39.5 us  [passed_along(): return lax.ppermute(x, axis, pairs)]
  transfers between devices with their start and end apart: 12 -> 8, of which waited for: 9 -> 2; matrix products, arithmetic and copies ran while one was open for 1% -> 0% of each run, Pallas kernels for 0% -> 22%
where the time goes in v1:
time: 119 us; the launch traced here: 117 us
  starting transfers between devices  39.5 us (33%)
  Pallas kernels  36.8 us (31%)
  blocking collectives  36.6 us (31%)
  waiting for transfers between devices  1.87 us (2%)
  local copies, waits for them, and re-layouts  1.3 us (1%)
    ppermute x8, starting transfers between devices, passed_along(): return lax.ppermute(x, axis, pairs)  39.5 us
    all_to_all x1, blocking collectives, per_device(): moments = lax.all_to_all(moments, ('region', 'tile'), 0, 0)  36.6 us
    pallas_call x2, Pallas kernels, self_part(): pl.pallas_call(self_kernel, out_shape=field, in_specs=[vmem] * 2, out_spe...  13.7 us
    pallas_call x2, Pallas kernels, inner_part(): pl.pallas_call(functools.partial(inner_kernel, (rows, cols)), out_shape=f...  11.6 us
    pallas_call x2, Pallas kernels, cross_part(): pl.pallas_call(functools.partial(cross_kernel, (rows, cols), last), out_s...  10.3 us
  transfers between devices with their start and end apart: 8, of which 2 were waited for; matrix products, arithmetic and copies ran while one was open for 0% of the time, Pallas kernels for 22%

profile of v1, /device:TPU:0, one launch (start us, length us, event | category | flops | bytes accessed | tf_op | source)
XLA Modules:
  0.0 117.0 jit_solution(4242353042599684354)
XLA Ops:
  0.6 0.0 copy-start.1
  0.6 1.1 constant_dynamic-update-slice_fusion.1
  1.7 0.0 copy-done.1
  1.8 1.3 %collective-permute-start.1 = (f32[4,34,256]{2,1,0:T(8,128)S(1)}, f32[4,34,256]{2,1,0:T(8,128)S(1)}, u32[]{:S(2)}, u32[]{:S(2)}) collective-permute-start(f32[4,34,256]{2,1,0:T(8,128)S(1)} %get-tuple-element.12), channel_id=1, source_target_pairs={{1,0},{2,1},{3,2},{4,3},{5,4},{6,5},{7,6},{9,8},{10,9},{11,10},{12... | collective-permute-start | bytes 417800 | tf_op jit(solution)/shard_map/ppermute | solution.py:286
  3.1 3.0 %collective-permute-start = (f32[4,34,256]{2,1,0:T(8,128)S(1)}, f32[4,34,256]{2,1,0:T(8,128)S(1)}, u32[]{:S(2)}, u32[]{:S(2)}) collective-permute-start(f32[4,34,256]{2,1,0:T(8,128)S(1)} %get-tuple-element.13), channel_id=1, source_target_pairs={{0,1},{1,2},{2,3},{3,4},{4,5},{5,6},{6,7},{8,9},{9,10},{10,11},{11... | collective-permute-start | bytes 417800 | tf_op jit(solution)/shard_map/ppermute | solution.py:286
  6.2 0.0 collective-permute-done.1.refs_4_.refs_8_
  6.2 0.9 collective-permute-done.refs_3_.refs_7_
  7.1 0.0 copy-start
  7.2 5.0 %collective-permute-start.2 = (f32[6,34,256]{2,1,0:T(8,128)S(1)}, f32[6,34,256]{2,1,0:T(8,128)S(1)}, u32[]{:S(2)}, u32[]{:S(2)}) collective-permute-start(f32[6,34,256]{2,1,0:T(8,128)S(1)} %pad_maximum_fusion), channel_id=1, source_target_pairs={{0,8},{8,16},{16,24},{1,9},{9,17},{17,25},{2,10},{10,18},{18,26},{... | collective-permute-start | bytes 626696 | tf_op jit(solution)/shard_map/ppermute | solution.py:286
  12.2 0.0 copy-start.2
  12.2 1.3 %collective-permute-start.3 = (f32[6,34,256]{2,1,0:T(8,128)S(1)}, f32[6,34,256]{2,1,0:T(8,128)S(1)}, u32[]{:S(2)}, u32[]{:S(2)}) collective-permute-start(f32[6,34,256]{2,1,0:T(8,128)S(1)} %pad_maximum_fusion.1), channel_id=1, source_target_pairs={{8,0},{16,8},{24,16},{9,1},{17,9},{25,17},{10,2},{18,10},{26,18},{... | collective-permute-start | bytes 626696 | tf_op jit(solution)/shard_map/ppermute | solution.py:286
  13.5 0.0 copy-done.2
  13.6 0.1 copy.18.pair_ref.refs_0_
  13.6 0.0 copy-done
  13.6 6.8 %own_blocks.2.sum_ref = f32[16,32,256]{2,1,0:T(8,128)S(1)} custom-call(f32[16,32,256]{2,1,0:T(8,128)S(1)} %bitcast.30, f32[16,2,256]{2,1,0:T(2,128)S(1)} %bitcast.35), custom_call_target="tpu_custom_call" | custom-call | flops 201326592 | bytes 2097152 | tf_op jit(solution)/shard_map/own_blocks/pallas_call | solution.py:322
  20.5 5.8 %inner_pairs.2.refs_2_ = f32[16,32,256]{2,1,0:T(8,128)S(1)} custom-call(s32[8,16]{1,0:T(8,128)S(1)} %copy.18.pair_ref.refs_0_, f32[16,32,256]{2,1,0:T(8,128)S(1)} %bitcast.31, f32[16,2,256]{2,1,0:T(2,128)S(1)} %bitcast.36, f32[16,32,256]{2,1,0:T(8,128)S(1)} %own_blocks.2.sum_ref), custom_call_target="tpu_custom_call" | custom-call | flops 603979776 | bytes 2097152 | tf_op jit(solution)/shard_map/inner_pairs/pallas_call | solution.py:328
  26.3 0.0 collective-permute-done.2.refs_5_.refs_9_
  26.3 0.0 collective-permute-done.3.refs_6_.refs_10_
  26.3 4.9 %cross_pairs.2.v_ref.refs_12_.v1_ref = f32[16,32,256]{2,1,0:T(8,128)S(1)} custom-call(s32[8,16]{1,0:T(8,128)S(1)} %copy.18.pair_ref.refs_0_, f32[16,2,256]{2,1,0:T(2,128)S(1)} %bitcast.37, f32[16,32,256]{2,1,0:T(8,128)S(1)} %inner_pairs.2.refs_2_, f32[4,34,256]{2,1,0:T(8,128)S(1)} %collective-permute-done.refs_3_.refs_7_, ...), custom_call_target="tpu_custom_call" | custom-call | flops 402653184 | bytes 2097152 | tf_op jit(solution)/shard_map/cross_pairs/pallas_call | solution.py:337
  31.2 1.3 %collective-permute-start.5 = (f32[4,32,256]{2,1,0:T(8,128)S(1)}, f32[4,32,256]{2,1,0:T(8,128)S(1)}, u32[]{:S(2)}, u32[]{:S(2)}) collective-permute-start(f32[4,32,256]{2,1,0:T(8,128)S(1)} %get-tuple-element.16), channel_id=1, source_target_pairs={{1,0},{2,1},{3,2},{4,3},{5,4},{6,5},{7,6},{9,8},{10,9},{11,10},{12... | collective-permute-start | bytes 393224 | tf_op jit(solution)/shard_map/ppermute | solution.py:286
  32.5 5.2 %collective-permute-start.4 = (f32[4,32,256]{2,1,0:T(8,128)S(1)}, f32[4,32,256]{2,1,0:T(8,128)S(1)}, u32[]{:S(2)}, u32[]{:S(2)}) collective-permute-start(f32[4,32,256]{2,1,0:T(8,128)S(1)} %get-tuple-element.17), channel_id=1, source_target_pairs={{0,1},{1,2},{2,3},{3,4},{4,5},{5,6},{6,7},{8,9},{9,10},{10,11},{11... | collective-permute-start | bytes 393224 | tf_op jit(solution)/shard_map/ppermute | solution.py:286
  37.7 0.0 collective-permute-done.5.refs_4_
  37.7 0.9 collective-permute-done.4.refs_3_
  38.7 21.1 %collective-permute-start.6 = (f32[6,32,256]{2,1,0:T(8,128)S(1)}, f32[6,32,256]{2,1,0:T(8,128)S(1)}, u32[]{:S(2)}, u32[]{:S(2)}) collective-permute-start(f32[6,32,256]{2,1,0:T(8,128)S(1)} %pad_maximum_fusion.2), channel_id=1, source_target_pairs={{0,8},{8,16},{16,24},{1,9},{9,17},{17,25},{2,10},{10,18},{18,26},{... | collective-permute-start | bytes 589832 | tf_op jit(solution)/shard_map/ppermute | solution.py:286
  59.8 1.3 %collective-permute-start.7 = (f32[6,32,256]{2,1,0:T(8,128)S(1)}, f32[6,32,256]{2,1,0:T(8,128)S(1)}, u32[]{:S(2)}, u32[]{:S(2)}) collective-permute-start(f32[6,32,256]{2,1,0:T(8,128)S(1)} %pad_maximum_fusion.3), channel_id=1, source_target_pairs={{8,0},{16,8},{24,16},{9,1},{17,9},{25,17},{10,2},{18,10},{26,18},{... | collective-permute-start | bytes 589832 | tf_op jit(solution)/shard_map/ppermute | solution.py:286
  61.1 6.8 %own_blocks.3.sum_ref = f32[16,32,256]{2,1,0:T(8,128)S(1)} custom-call(f32[16,32,256]{2,1,0:T(8,128)S(1)} %cross_pairs.2.v_ref.refs_12_.v1_ref, f32[16,2,256]{2,1,0:T(2,128)S(1)} %bitcast.38), custom_call_target="tpu_custom_call" | custom-call | flops 201326592 | bytes 2097152 | tf_op jit(solution)/shard_map/own_blocks/pallas_call | solution.py:322
  68.0 5.8 %inner_pairs.3.refs_2_ = f32[16,32,256]{2,1,0:T(8,128)S(1)} custom-call(s32[8,16]{1,0:T(8,128)S(1)} %copy.18.pair_ref.refs_0_, f32[16,32,256]{2,1,0:T(8,128)S(1)} %cross_pairs.2.v_ref.refs_12_.v1_ref, f32[16,2,256]{2,1,0:T(2,128)S(1)} %bitcast.39, f32[16,32,256]{2,1,0:T(8,128)S(1)} %own_blocks.3.sum_ref), custom_call_target="tpu_custom_call" | custom-call | flops 603979776 | bytes 2097152 | tf_op jit(solution)/shard_map/inner_pairs/pallas_call | solution.py:328
  73.7 0.0 collective-permute-done.6.refs_5_
  73.8 0.0 collective-permute-done.7.refs_6_
  73.8 5.4 %cross_pairs.3 = (f32[16,32,256]{2,1,0:T(8,128)S(1)}, f32[32,1,128]{2,1,0:T(1,128)S(1)}) custom-call(s32[8,16]{1,0:T(8,128)S(1)} %copy.18.pair_ref.refs_0_, f32[16,2,256]{2,1,0:T(2,128)S(1)} %bitcast.40, f32[16,32,256]{2,1,0:T(8,128)S(1)} %inner_pairs.3.refs_2_, f32[4,32,256]{2,1,0:T(8,128)S(1)} %collective-permute-done.4.refs_3_, ...), custom_call_target="tpu_custom_call" | custom-call | flops 402653184 | bytes 2097152 | tf_op jit(solution)/shard_map/cross_pairs/pallas_call | solution.py:337
  79.2 36.6 %all_to_all.5.moments_ref = f32[32,1,128]{2,1,0:T(1,128)S(1)} all-to-all(f32[32,1,128]{2,1,0:T(1,128)S(1)} %get-tuple-element.6), channel_id=1, replica_groups=mesh['region'=4,'tile'=8] {'region','tile'}, dimensions={0} | all-to-all | bytes 32768 | tf_op jit(solution)/shard_map/all_to_all | solution.py:359
  115.8 1.3 %final_update.1 = (f32[16,32,256]{2,1,0:T(8,128)}, f32[16,32,256]{2,1,0:T(8,128)}) custom-call(f32[32,1,128]{2,1,0:T(1,128)S(1)} %all_to_all.5.moments_ref, f32[16,32,256]{2,1,0:T(8,128)S(1)} %bitcast.33, f32[16,32,256]{2,1,0:T(8,128)S(1)} %cross_pairs.2.v_ref.refs_12_.v1_ref, f32[16,32,256]{2,1,0:T(8,128)S(1)} %get-tuple-element.7.v2_ref), custom_call_target="tpu_custom_call" | custom-call | tf_op jit(solution)/shard_map/final_update/pallas_call | solution.py:360
  (13 shorter events, 0.2 us)
Async XLA Ops:
  0.6 1.1 copy-start.1
  1.8 4.4 %collective-permute-start.1 = (f32[4,34,256]{2,1,0:T(8,128)S(1)}, f32[4,34,256]{2,1,0:T(8,128)S(1)}, u32[]{:S(2)}, u32[]{:S(2)}) collective-permute-start(f32[4,34,256]{2,1,0:T(8,128)S(1)} %get-tuple-element.12), channel_id=1, source_target_pairs={{1,0},{2,1},{3,2},{4,3},{5,4},{6,5},{7,6},{9,8},{10,9},{11,10},{12... | collective-permute-start | bytes 417800 | tf_op jit(solution)/shard_map/ppermute | solution.py:286
  3.1 4.0 %collective-permute-start = (f32[4,34,256]{2,1,0:T(8,128)S(1)}, f32[4,34,256]{2,1,0:T(8,128)S(1)}, u32[]{:S(2)}, u32[]{:S(2)}) collective-permute-start(f32[4,34,256]{2,1,0:T(8,128)S(1)} %get-tuple-element.13), channel_id=1, source_target_pairs={{0,1},{1,2},{2,3},{3,4},{4,5},{5,6},{6,7},{8,9},{9,10},{10,11},{11... | collective-permute-start | bytes 417800 | tf_op jit(solution)/shard_map/ppermute | solution.py:286
  7.1 6.5 %copy-start = (f32[4,4,32,256]{3,2,1,0:T(8,128)S(1)}, f32[4,4,32,256]{3,2,1,0:T(8,128)}, u32[]{:S(2)}) copy-start(f32[4,4,32,256]{3,2,1,0:T(8,128)} %param.3) | copy-start | bytes 1572868
  7.2 19.1 %collective-permute-start.2 = (f32[6,34,256]{2,1,0:T(8,128)S(1)}, f32[6,34,256]{2,1,0:T(8,128)S(1)}, u32[]{:S(2)}, u32[]{:S(2)}) collective-permute-start(f32[6,34,256]{2,1,0:T(8,128)S(1)} %pad_maximum_fusion), channel_id=1, source_target_pairs={{0,8},{8,16},{16,24},{1,9},{9,17},{17,25},{2,10},{10,18},{18,26},{... | collective-permute-start | bytes 626696 | tf_op jit(solution)/shard_map/ppermute | solution.py:286
  12.2 1.3 %copy-start.2 = (s32[8,4,4]{0,2,1:T(4,128)S(1)}, s32[8,4,4]{0,2,1:T(4,128)}, u32[]{:S(2)}) copy-start(s32[8,4,4]{0,2,1:T(4,128)} %param.5) | copy-start | bytes 1540
  12.2 14.0 %collective-permute-start.3 = (f32[6,34,256]{2,1,0:T(8,128)S(1)}, f32[6,34,256]{2,1,0:T(8,128)S(1)}, u32[]{:S(2)}, u32[]{:S(2)}) collective-permute-start(f32[6,34,256]{2,1,0:T(8,128)S(1)} %pad_maximum_fusion.1), channel_id=1, source_target_pairs={{8,0},{16,8},{24,16},{9,1},{17,9},{25,17},{10,2},{18,10},{26,18},{... | collective-permute-start | bytes 626696 | tf_op jit(solution)/shard_map/ppermute | solution.py:286
  31.2 6.5 %collective-permute-start.5 = (f32[4,32,256]{2,1,0:T(8,128)S(1)}, f32[4,32,256]{2,1,0:T(8,128)S(1)}, u32[]{:S(2)}, u32[]{:S(2)}) collective-permute-start(f32[4,32,256]{2,1,0:T(8,128)S(1)} %get-tuple-element.16), channel_id=1, source_target_pairs={{1,0},{2,1},{3,2},{4,3},{5,4},{6,5},{7,6},{9,8},{10,9},{11,10},{12... | collective-permute-start | bytes 393224 | tf_op jit(solution)/shard_map/ppermute | solution.py:286
  32.5 6.2 %collective-permute-start.4 = (f32[4,32,256]{2,1,0:T(8,128)S(1)}, f32[4,32,256]{2,1,0:T(8,128)S(1)}, u32[]{:S(2)}, u32[]{:S(2)}) collective-permute-start(f32[4,32,256]{2,1,0:T(8,128)S(1)} %get-tuple-element.17), channel_id=1, source_target_pairs={{0,1},{1,2},{2,3},{3,4},{4,5},{5,6},{6,7},{8,9},{9,10},{10,11},{11... | collective-permute-start | bytes 393224 | tf_op jit(solution)/shard_map/ppermute | solution.py:286
  38.7 35.1 %collective-permute-start.6 = (f32[6,32,256]{2,1,0:T(8,128)S(1)}, f32[6,32,256]{2,1,0:T(8,128)S(1)}, u32[]{:S(2)}, u32[]{:S(2)}) collective-permute-start(f32[6,32,256]{2,1,0:T(8,128)S(1)} %pad_maximum_fusion.2), channel_id=1, source_target_pairs={{0,8},{8,16},{16,24},{1,9},{9,17},{17,25},{2,10},{10,18},{18,26},{... | collective-permute-start | bytes 589832 | tf_op jit(solution)/shard_map/ppermute | solution.py:286
  59.8 14.0 %collective-permute-start.7 = (f32[6,32,256]{2,1,0:T(8,128)S(1)}, f32[6,32,256]{2,1,0:T(8,128)S(1)}, u32[]{:S(2)}, u32[]{:S(2)}) collective-permute-start(f32[6,32,256]{2,1,0:T(8,128)S(1)} %pad_maximum_fusion.3), channel_id=1, source_target_pairs={{8,0},{16,8},{24,16},{9,1},{17,9},{25,17},{10,2},{18,10},{26,18},{... | collective-permute-start | bytes 589832 | tf_op jit(solution)/shard_map/ppermute | solution.py:286

commit v2 on v1

v2 whole, which is shorter than its diff:
```python
import functools

import jax
import jax.numpy as jnp
from jax import lax
from jax.experimental import pallas as pl
from jax.experimental.pallas import tpu as pltpu
from jax.sharding import PartitionSpec as P

LENGTH_SCALE = 0.2
TAPER_RANGE = 0.5
NUGGET = 3.0
OFFSETS = ((0, 1), (1, 0), (1, 1), (1, -1), (0, -1), (-1, 0), (-1, -1), (-1, 1))
UNIT = 1.4426950408889634 / LENGTH_SCALE
EDGE = UNIT * TAPER_RANGE
WEIGHT = 4.0 * 2.0**-EDGE / EDGE**5
STRIP = 64
VMEM_LIMIT = 10 * 1024 * 1024


def dot_nn(a, b):
    return lax.dot_general(a, b, (((1,), (0,)), ((), ())), preferred_element_type=jnp.float32)


def dot_nt(a, b):
    return lax.dot_general(a, b, (((1,), (1,)), ((), ())), preferred_element_type=jnp.float32)


def split_hi_lo(values):
    hi = values.astype(jnp.bfloat16)
    lo = (values - hi.astype(jnp.float32)).astype(jnp.bfloat16)
    return hi, lo


def across_lanes(row, lanes):
    return jnp.transpose(jnp.broadcast_to(row, (lanes, row.shape[1])))


def spread_points(spread_ref, at, points):
    tall = jnp.transpose(jnp.concatenate([points * UNIT] * 4, axis=0))
    for axis in range(2):
        spread_ref[at, axis] = jnp.broadcast_to(tall[:, axis : axis + 1], spread_ref.shape[2:])


def make_tile(tile_ref, keep_ref, slot, spread_ref, other, points_ref, own, shift_a, shift_b):
    points = tile_ref.shape[1]
    lanes = spread_ref.shape[3]
    own_x = points_ref[own, 0:1] - shift_a
    own_y = points_ref[own, 1:2] - shift_b
    for start in range(0, points, STRIP):
        rows = slice(start, start + STRIP)
        for left in range(0, points, lanes):
            cols = slice(left, left + lanes)
            gap_x = spread_ref[other, 0, rows] - own_x[:, cols]
            gap_y = spread_ref[other, 1, rows] - own_y[:, cols]
            square = jnp.maximum(gap_x * gap_x + gap_y * gap_y, 1e-30)
            rest = jnp.maximum(EDGE - square * lax.rsqrt(square), 0.0)
            rest2 = rest * rest
            cov = (jnp.exp2(rest) * (rest2 * rest2)) * (1.25 * EDGE - rest)
            for part, values in enumerate(split_hi_lo(cov)):
                tile_ref[part, rows, cols] = values
                keep_ref[slot, part, rows, cols] = values


def product(dot, parts_ref, at, high, low):
    rhs = parts_ref.shape[1] // 2
    both = dot(parts_ref[at], high)
    cross = dot(parts_ref[at, 0:rhs], low)
    return both[:rhs] + both[rhs:] + cross


def store_parts(parts_ref, at, values):
    rhs = values.shape[0]
    hi, lo = split_hi_lo(values * WEIGHT)
    parts_ref[at, 0:rhs] = hi
    parts_ref[at, rhs : 2 * rhs] = lo


def make_and_use(turns, item_at, tile_a, tile_b, make, use):
    tile_b[...] = jnp.zeros_like(tile_b)

    def one_turn(turn, carry):
        use(tile_b[0], tile_b[1], item_at(2 * turn))
        make(tile_a, 2 * turn, item_at(2 * turn + 1))
        use(tile_a[0], tile_a[1], item_at(2 * turn + 1))
        make(tile_b, 2 * turn + 1, item_at(2 * turn + 2))
        return carry

    lax.fori_loop(0, turns, one_turn, 0)
    use(tile_b[0], tile_b[1], item_at(2 * turns))


def only_use(turns, item_at, kept_ref, base, use):
    def one_turn(turn, carry):
        for half in range(2):
            slot = base + 2 * turn + half
            use(kept_ref[slot, 0], kept_ref[slot, 1], item_at(2 * turn + half + 1))
        return carry

    lax.fori_loop(0, turns, one_turn, 0)


def item_code(own, other, shift_a, shift_b):
    return own + 64 * other + 4096 * (shift_a + 1) + 16384 * (shift_b + 1)


NO_ITEM = item_code(0, 0, 2, 2)


def item_blocks(code):
    return lax.bitwise_and(code, 63), lax.bitwise_and(lax.shift_right_logical(code, 6), 63)


def item_shifts(code):
    shift_a = lax.bitwise_and(lax.shift_right_logical(code, 12), 3) - 1
    shift_b = lax.shift_right_logical(code, 14) - 1
    return shift_a.astype(jnp.float32) * UNIT, shift_b.astype(jnp.float32) * UNIT


def list_items(items_ref, candidates, pair_ref):
    items_ref[0] = NO_ITEM
    count = jnp.int32(0)
    for k, own, code in candidates:
        items_ref[count + 1] = code
        count = count + jnp.where(pair_ref[k, own] > 0, 1, 0)
    items_ref[count + 1] = NO_ITEM
    items_ref[count + 2] = NO_ITEM
    return lax.shift_right_logical(count + 1, 1)


def inner_candidates(rows, cols):
    found = []
    for k in range(4):
        shift_a, shift_b = OFFSETS[k]
        for a in range(rows):
            for b in range(cols):
                if 0 <= a + shift_a < rows and 0 <= b + shift_b < cols:
                    own = a * cols + b
                    other = own + shift_a * cols + shift_b
                    found.append((k, own, item_code(own, other, shift_a, shift_b)))
    return found


def cross_candidates(rows, cols):
    places = [(a, -1) for a in range(rows)] + [(a, cols) for a in range(rows)]
    places += [(-1, b) for b in range(-1, cols + 1)] + [(rows, b) for b in range(-1, cols + 1)]
    found = []
    for k in range(8):
        shift_a, shift_b = OFFSETS[k]
        for a in range(rows):
            for b in range(cols):
                place = (a + shift_a, b + shift_b)
                if place in places:
                    own = a * cols + b
                    found.append((k, own, item_code(own, places.index(place), shift_a, shift_b)))
    return found


def near_kernel(shape, again, pair_ref, *refs):
    blocks = shape[0] * shape[1]
    if again:
        v_ref, kept_ref, out_ref, items_ref, parts_ref = refs
    else:
        v_ref, c_ref, out_ref, kept_ref, items_ref, parts_ref, points_ref, spread_ref, tile_a, tile_b = refs

    def prepare(at, carry):
        store_parts(parts_ref, at, v_ref[at])
        out_ref[at] = NUGGET * v_ref[at]
        if not again:
            points_ref[at] = c_ref[at] * UNIT
            spread_points(spread_ref, at, c_ref[at])
        return carry

    lax.fori_loop(0, blocks, prepare, 0)
    turns = list_items(items_ref, inner_candidates(*shape), pair_ref)

    def own_item(n):
        return jnp.maximum(n - 1, 0)

    def use_own(high, low, at):
        out_ref[at] += product(dot_nn, parts_ref, at, high, low)

    def use(high, low, code):
        own, other = item_blocks(code)
        out_ref[own] += product(dot_nn, parts_ref, other, high, low)
        out_ref[other] += product(dot_nt, parts_ref, own, high, low)

    if again:
        only_use(blocks // 2, own_item, kept_ref, 0, use_own)
        only_use(turns, lambda n: items_ref[n], kept_ref, blocks, use)
        return

    def make_own(tile_ref, slot, at):
        make_tile(tile_ref, kept_ref, slot, spread_ref, at, points_ref, at, 0.0, 0.0)

    def make(tile_ref, slot, code):
        own, other = item_blocks(code)
        make_tile(tile_ref, kept_ref, blocks + slot, spread_ref, other, points_ref, own, *item_shifts(code))

    make_and_use(blocks // 2, own_item, tile_a, tile_b, make_own, use_own)
    make_and_use(turns, lambda n: items_ref[n], tile_a, tile_b, make, use)


def cross_kernel(shape, again, pair_ref, sum_ref, *refs):
    rows, cols = shape
    halo = refs[:4]
    if again:
        kept_ref, v0_ref, v1_ref, out_ref, moments_ref, items_ref, parts_ref = refs[4:]
    else:
        c_ref, out_ref, kept_ref, items_ref, parts_ref, points_ref, spread_ref, tile_a, tile_b = refs[4:]
    rhs = out_ref.shape[1]

    def prepare(at, carry):
        out_ref[at] = sum_ref[at]
        if not again:
            points_ref[at] = c_ref[at] * UNIT
        return carry

    lax.fori_loop(0, rows * cols, prepare, 0)
    turns = list_items(items_ref, cross_candidates(rows, cols), pair_ref)
    start = 0
    for side in halo:

        def take(at, carry, side=side, start=start):
            store_parts(parts_ref, start + at, side[at, 0:rhs])
            if not again:
                spread_points(spread_ref, start + at, side[at, rhs : rhs + 2])
            return carry

        lax.fori_loop(0, side.shape[0], take, 0)
        start += side.shape[0]

    def use(high, low, code):
        own, other = item_blocks(code)
        out_ref[own] += product(dot_nn, parts_ref, other, high, low)

    if not again:

        def make(tile_ref, slot, code):
            own, other = item_blocks(code)
            make_tile(tile_ref, kept_ref, slot, spread_ref, other, points_ref, own, *item_shifts(code))

        make_and_use(turns, lambda n: items_ref[n], tile_a, tile_b, make, use)
        return

    only_use(turns, lambda n: items_ref[n], kept_ref, 0, use)
    zero = jnp.zeros(out_ref.shape[1:], jnp.float32)

    def gather(at, sums):
        w0, w1, w2 = v0_ref[at], v1_ref[at], out_ref[at]
        terms = (w0 * w0, w0 * w1, w1 * w1, w1 * w2)
        return tuple(s + t for s, t in zip(sums, terms))

    sums = lax.fori_loop(0, rows * cols, gather, (zero,) * 4)
    lanes = moments_ref.shape[2]
    folded = [sum(s[:, left : left + lanes] for left in range(0, s.shape[1], lanes)) for s in sums]
    stacked = jnp.concatenate(folded, axis=0)
    line = jnp.sum(jnp.transpose(stacked), axis=0, keepdims=True)
    moments_ref[...] = jnp.broadcast_to(line[None], moments_ref.shape)


def final_kernel(moments_ref, v0_ref, v1_ref, v2_ref, solution_ref, residual_ref):
    rhs, points = v0_ref.shape[1:]
    line = moments_ref[0]
    for at in range(1, moments_ref.shape[0]):
        line = line + moments_ref[at]
    table = across_lanes(line, line.shape[1])
    m00, m01, m11, m12 = (table[k * rhs : (k + 1) * rhs] for k in range(4))
    a = m00 / m01
    norm = m00 - 2.0 * a * m01 + a * a * m11
    grow = 1.0 + norm / m00
    step = norm / (grow * (grow * m01 - 2.0 * a * m11) + a * a * m12)
    first = jnp.concatenate([a + step * grow] * (points // line.shape[1]), axis=1)
    second = jnp.concatenate([step * a] * (points // line.shape[1]), axis=1)

    def one(at, carry):
        w0, w1, w2 = v0_ref[at], v1_ref[at], v2_ref[at]
        solution_ref[at] = first * w0 - second * w1
        residual_ref[at] = w0 - first * w1 + second * w2
        return carry

    lax.fori_loop(0, v0_ref.shape[0], one, 0)


def passed_along(x, axis, by):
    count = lax.axis_size(axis)
    pairs = [(i, i + by) for i in range(count) if 0 <= i + by < count]
    return lax.ppermute(x, axis, pairs)


def per_device(right_side, coords, pair_list):
    rows, cols, rhs, points = right_side.shape
    blocks = rows * cols
    devices = lax.axis_size("region") * lax.axis_size("tile")
    lanes = 128
    f32 = jnp.float32
    halo = 2 * rows + 2 * (cols + 2)
    near_count = len(inner_candidates(rows, cols))
    cross_count = len(cross_candidates(rows, cols))
    pairs = pair_list.reshape(8, blocks)
    own_points = coords.reshape(blocks, 2, points)
    field = jax.ShapeDtypeStruct((blocks, rhs, points), f32)
    vmem = pl.BlockSpec(memory_space=pltpu.VMEM)
    smem = pl.BlockSpec(memory_space=pltpu.SMEM)

    def tiles(count):
        return jax.ShapeDtypeStruct((count, 2, points, points), jnp.bfloat16)

    def call(kernel, name, inputs, outputs, listed, others, again, count):
        scratch = [pltpu.SMEM((listed + 3,), jnp.int32), pltpu.VMEM((others, 2 * rhs, points), jnp.bfloat16)]
        if not again:
            scratch += [pltpu.VMEM((blocks, 2, points), f32), pltpu.VMEM((others, 2, points, lanes), f32)]
            scratch += [pltpu.VMEM((2, points, points), jnp.bfloat16)] * 2
        return pl.pallas_call(
            functools.partial(kernel, (rows, cols), again), out_shape=outputs,
            in_specs=[smem] + [vmem] * len(inputs), out_specs=(vmem,) * len(outputs), scratch_shapes=scratch,
            compiler_params=pltpu.CompilerParams(vmem_limit_bytes=VMEM_LIMIT), name=name,
            cost_estimate=pl.CostEstimate(
                flops=count * 6 * rhs * points * points, transcendentals=0 if again else count * 2 * points * points,
                bytes_accessed=count * 4 * points * points,
            ),
        )(pairs, *inputs)

    def exchange(packed):
        prev_col = passed_along(packed[:, cols - 1], "tile", 1)
        next_col = passed_along(packed[:, 0], "tile", -1)
        top = jnp.concatenate([prev_col[:1], packed[0], next_col[:1]], axis=0)
        bottom = jnp.concatenate([prev_col[rows - 1 :], packed[rows - 1], next_col[rows - 1 :]], axis=0)
        return prev_col, next_col, passed_along(bottom, "region", 1), passed_along(top, "region", -1)

    w0 = right_side.reshape(blocks, rhs, points)
    round_w0 = exchange(jnp.concatenate([right_side, coords], axis=2))
    part, near_tiles = call(
        near_kernel, "near_first", (w0, own_points), (field, tiles(blocks + near_count + 2)),
        near_count, blocks, False, blocks + near_count,
    )
    w1, cross_tiles = call(
        cross_kernel, "cross_first", (part, *round_w0, own_points), (field, tiles(cross_count + 2)),
        cross_count, halo, False, cross_count,
    )
    round_w1 = exchange(w1.reshape(right_side.shape))
    (part,) = call(
        near_kernel, "near_again", (w1, near_tiles), (field,), near_count, blocks, True, blocks + near_count
    )
    w2, moments = call(
        cross_kernel, "cross_again", (part, *round_w1, cross_tiles, w0, w1),
        (field, jax.ShapeDtypeStruct((devices, 1, 4 * rhs), f32)), cross_count, halo, True, cross_count,
    )
    moments = lax.all_to_all(moments, ("region", "tile"), 0, 0)
    solution, residual = pl.pallas_call(
        final_kernel, out_shape=(field, field), in_specs=[vmem] * 4, out_specs=(vmem, vmem),
        compiler_params=pltpu.CompilerParams(vmem_limit_bytes=VMEM_LIMIT), name="final_update",
    )(moments, w0, w1, w2)
    return solution.reshape(right_side.shape), residual.reshape(right_side.shape)


def solution(mesh):
    placed = (
        P("region", "tile", None, None),
        P("region", "tile", None, None),
        P(None, "region", "tile"),
    )
    return jax.shard_map(
        per_device,
        mesh=mesh,
        in_specs=placed,
        out_specs=(P("region", "tile", None, None), P("region", "tile", None, None)),
        check_vma=False,
    )
```

time: 119 us -> 101 us (0.85)
  starting transfers between devices: 39.5 us -> 17.4 us
  Pallas kernels: 36.8 us -> 51.3 us
  blocking collectives: 36.6 us -> 23.7 us
  local copies, waits for them, and re-layouts: 1.3 us -> 4.55 us
    ppermute x8, starting transfers between devices: 39.5 us -> 17.4 us  [passed_along(): return lax.ppermute(x, axis, pairs)]
    pallas_call x6 -> x4, Pallas kernels: 35.5 us -> 50 us  [call(): pl.pallas_call(functools.partial(kernel, (rows, cols), again), out_shape=...]
    all_to_all x1, blocking collectives: 36.6 us -> 23.7 us  [per_device(): moments = lax.all_to_all(moments, ('region', 'tile'), 0, 0)]
    unnamed x7 -> x9, local copies, waits for them, and re-layouts: 1.1 us -> 2.89 us
  transfers between devices with their start and end apart: 8 -> 8, of which waited for: 2 -> 2; matrix products, arithmetic and copies ran while one was open for 0% -> 1% of each run, Pallas kernels for 22% -> 34%
where the time goes in v2:
time: 101 us; the launch traced here: 99.8 us
  Pallas kernels  51.3 us (51%)
  blocking collectives  23.7 us (23%)
  starting transfers between devices  17.4 us (17%)
  local copies, waits for them, and re-layouts  4.55 us (5%)
  waiting for transfers between devices  1.87 us (2%)
    pallas_call x4, Pallas kernels, call(): pl.pallas_call(functools.partial(kernel, (rows, cols), again), out_shape=...  50 us
    all_to_all x1, blocking collectives, per_device(): moments = lax.all_to_all(moments, ('region', 'tile'), 0, 0)  23.7 us
    ppermute x8, starting transfers between devices, passed_along(): return lax.ppermute(x, axis, pairs)  17.4 us
    unnamed x9, local copies, waits for them, and re-layouts  2.89 us
  transfers between devices with their start and end apart: 8, of which 2 were waited for; matrix products, arithmetic and copies ran while one was open for 1% of the time, Pallas kernels for 34%

profile of v2, /device:TPU:0, one launch (start us, length us, event | category | flops | bytes accessed | tf_op | source)
XLA Modules:
  0.0 99.8 jit_solution(3344138090915926921)
XLA Ops:
  0.6 0.0 copy-start.3
  0.6 1.1 %constant_dynamic-update-slice_fusion.1 = f32[4,4,34,256]{3,2,1,0:T(8,128)S(1)} fusion(f32[4,4,32,256]{3,2,1,0:T(8,128)} %param.3), kind=kLoop, calls=%fused_computation.11 | loop fusion | bytes 1048576
  1.7 0.8 constant_dynamic-update-slice_fusion
  2.5 1.3 %collective-permute-start.1 = (f32[4,34,256]{2,1,0:T(8,128)S(1)}, f32[4,34,256]{2,1,0:T(8,128)S(1)}, u32[]{:S(2)}, u32[]{:S(2)}) collective-permute-start(f32[4,34,256]{2,1,0:T(8,128)S(1)} %get-tuple-element.20), channel_id=1, source_target_pairs={{1,0},{2,1},{3,2},{4,3},{5,4},{6,5},{7,6},{9,8},{10,9},{11,10},{12... | collective-permute-start | bytes 417800 | tf_op jit(solution)/shard_map/ppermute | solution.py:288
  3.8 3.0 %collective-permute-start = (f32[4,34,256]{2,1,0:T(8,128)S(1)}, f32[4,34,256]{2,1,0:T(8,128)S(1)}, u32[]{:S(2)}, u32[]{:S(2)}) collective-permute-start(f32[4,34,256]{2,1,0:T(8,128)S(1)} %get-tuple-element.21), channel_id=1, source_target_pairs={{0,1},{1,2},{2,3},{3,4},{4,5},{5,6},{6,7},{8,9},{9,10},{10,11},{11... | collective-permute-start | bytes 417800 | tf_op jit(solution)/shard_map/ppermute | solution.py:288
  6.9 0.0 collective-permute-done.1.refs_1_
  6.9 0.9 collective-permute-done.refs_0_
  7.9 4.9 %collective-permute-start.2 = (f32[6,34,256]{2,1,0:T(8,128)S(1)}, f32[6,34,256]{2,1,0:T(8,128)S(1)}, u32[]{:S(2)}, u32[]{:S(2)}) collective-permute-start(f32[6,34,256]{2,1,0:T(8,128)S(1)} %pad_maximum_fusion), channel_id=1, source_target_pairs={{0,8},{8,16},{16,24},{1,9},{9,17},{17,25},{2,10},{10,18},{18,26},{... | collective-permute-start | bytes 626696 | tf_op jit(solution)/shard_map/ppermute | solution.py:288
  12.8 1.3 %collective-permute-start.3 = (f32[6,34,256]{2,1,0:T(8,128)S(1)}, f32[6,34,256]{2,1,0:T(8,128)S(1)}, u32[]{:S(2)}, u32[]{:S(2)}) collective-permute-start(f32[6,34,256]{2,1,0:T(8,128)S(1)} %pad_maximum_fusion.1), channel_id=1, source_target_pairs={{8,0},{16,8},{24,16},{9,1},{17,9},{25,17},{10,2},{18,10},{26,18},{... | collective-permute-start | bytes 626696 | tf_op jit(solution)/shard_map/ppermute | solution.py:288
  14.1 0.8 copy.18.pair_ref
  14.9 0.0 copy-start
  14.9 1.0 %copy-done = f32[4,4,32,256]{3,2,1,0:T(8,128)S(1)} copy-done((f32[4,4,32,256]{3,2,1,0:T(8,128)S(1)}, f32[4,4,32,256]{3,2,1,0:T(8,128)}, u32[]{:S(2)}) %copy-start) | copy-done | bytes 524312
  16.0 0.0 copy-start.2
  16.0 0.8 copy-done.2
  16.7 23.7 %near_first.1 = (f32[16,32,256]{2,1,0:T(8,128)S(1)}, bf16[60,2,256,256]{3,2,1,0:T(8,128)(2,1)S(1)}) custom-call(s32[8,16]{1,0:T(8,128)S(1)} %copy.18.pair_ref, f32[16,32,256]{2,1,0:T(8,128)S(1)} %bitcast.31, f32[16,2,256]{2,1,0:T(2,128)S(1)} %bitcast.34), custom_call_target="tpu_custom_call" | custom-call | flops 729808896 | bytes 15204352 | tf_op jit(solution)/shard_map/near_first/pallas_call | solution.py:314
  40.4 0.0 copy-start.1
  40.4 0.0 collective-permute-done.2.refs_2_
  40.5 0.0 collective-permute-done.3.refs_3_
  40.5 0.0 copy-done.3
  40.5 12.7 %cross_first.1 = (f32[16,32,256]{2,1,0:T(8,128)S(1)}, bf16[46,2,256,256]{3,2,1,0:T(8,128)(2,1)S(1)}) custom-call(s32[8,16]{1,0:T(8,128)S(1)} %copy.18.pair_ref, f32[16,32,256]{2,1,0:T(8,128)S(1)} %get-tuple-element.10.sum_ref, f32[4,34,256]{2,1,0:T(8,128)S(1)} %collective-permute-done.refs_0_, f32[4,34,256]{2,1,0:T(8,128)S(1)} %collective-permute-done.1.refs_1_, ...), custom_call_target="tpu_custom_call" | custom-call | flops 553648128 | bytes 11534336 | tf_op jit(solution)/shard_map/cross_first/pallas_call | solution.py:314
  53.2 1.3 %collective-permute-start.5 = (f32[4,32,256]{2,1,0:T(8,128)S(1)}, f32[4,32,256]{2,1,0:T(8,128)S(1)}, u32[]{:S(2)}, u32[]{:S(2)}) collective-permute-start(f32[4,32,256]{2,1,0:T(8,128)S(1)} %get-tuple-element.24), channel_id=1, source_target_pairs={{1,0},{2,1},{3,2},{4,3},{5,4},{6,5},{7,6},{9,8},{10,9},{11,10},{12... | collective-permute-start | bytes 393224 | tf_op jit(solution)/shard_map/ppermute | solution.py:288
  54.5 3.0 %collective-permute-start.4 = (f32[4,32,256]{2,1,0:T(8,128)S(1)}, f32[4,32,256]{2,1,0:T(8,128)S(1)}, u32[]{:S(2)}, u32[]{:S(2)}) collective-permute-start(f32[4,32,256]{2,1,0:T(8,128)S(1)} %get-tuple-element.25), channel_id=1, source_target_pairs={{0,1},{1,2},{2,3},{3,4},{4,5},{5,6},{6,7},{8,9},{9,10},{10,11},{11... | collective-permute-start | bytes 393224 | tf_op jit(solution)/shard_map/ppermute | solution.py:288
  57.6 0.0 collective-permute-done.5.refs_1_
  57.6 0.9 collective-permute-done.4.refs_0_
  58.5 1.3 %collective-permute-start.6 = (f32[6,32,256]{2,1,0:T(8,128)S(1)}, f32[6,32,256]{2,1,0:T(8,128)S(1)}, u32[]{:S(2)}, u32[]{:S(2)}) collective-permute-start(f32[6,32,256]{2,1,0:T(8,128)S(1)} %pad_maximum_fusion.2), channel_id=1, source_target_pairs={{0,8},{8,16},{16,24},{1,9},{9,17},{17,25},{2,10},{10,18},{18,26},{... | collective-permute-start | bytes 589832 | tf_op jit(solution)/shard_map/ppermute | solution.py:288
  59.9 1.3 %collective-permute-start.7 = (f32[6,32,256]{2,1,0:T(8,128)S(1)}, f32[6,32,256]{2,1,0:T(8,128)S(1)}, u32[]{:S(2)}, u32[]{:S(2)}) collective-permute-start(f32[6,32,256]{2,1,0:T(8,128)S(1)} %pad_maximum_fusion.3), channel_id=1, source_target_pairs={{8,0},{16,8},{24,16},{9,1},{17,9},{25,17},{10,2},{18,10},{26,18},{... | collective-permute-start | bytes 589832 | tf_op jit(solution)/shard_map/ppermute | solution.py:288
  61.2 10.1 %near_again.1.sum_ref = f32[16,32,256]{2,1,0:T(8,128)S(1)} custom-call(s32[8,16]{1,0:T(8,128)S(1)} %copy.18.pair_ref, f32[16,32,256]{2,1,0:T(8,128)S(1)} %get-tuple-element.11.refs_0_.refs_6_.v1_ref, bf16[60,2,256,256]{3,2,1,0:T(8,128)(2,1)S(1)} %get-tuple-element.12.refs_1_), custom_call_target="tpu_custom_call" | custom-call | flops 729808896 | bytes 15204352 | tf_op jit(solution)/shard_map/near_again/pallas_call | solution.py:314
  71.3 0.0 collective-permute-done.6.refs_2_
  71.3 0.0 collective-permute-done.7.refs_3_
  71.3 0.0 copy-done.1
  71.3 3.5 %cross_again.1 = (f32[16,32,256]{2,1,0:T(8,128)S(1)}, f32[32,1,128]{2,1,0:T(1,128)S(1)}) custom-call(s32[8,16]{1,0:T(8,128)S(1)} %copy.18.pair_ref, f32[16,32,256]{2,1,0:T(8,128)S(1)} %near_again.1.sum_ref, f32[4,32,256]{2,1,0:T(8,128)S(1)} %collective-permute-done.4.refs_0_, f32[4,32,256]{2,1,0:T(8,128)S(1)} %collective-permute-done.5.refs_1_, ...), custom_call_target="tpu_custom_call" | custom-call | flops 553648128 | bytes 11534336 | tf_op jit(solution)/shard_map/cross_again/pallas_call | solution.py:314
  74.8 23.7 %all_to_all.5.moments_ref = f32[32,1,128]{2,1,0:T(1,128)S(1)} all-to-all(f32[32,1,128]{2,1,0:T(1,128)S(1)} %get-tuple-element.14), channel_id=1, replica_groups=mesh['region'=4,'tile'=8] {'region','tile'}, dimensions={0} | all-to-all | bytes 32768 | tf_op jit(solution)/shard_map/all_to_all | solution.py:349
  98.6 1.3 %final_update.1 = (f32[16,32,256]{2,1,0:T(8,128)}, f32[16,32,256]{2,1,0:T(8,128)}) custom-call(f32[32,1,128]{2,1,0:T(1,128)S(1)} %all_to_all.5.moments_ref, f32[16,32,256]{2,1,0:T(8,128)S(1)} %bitcast.33, f32[16,32,256]{2,1,0:T(8,128)S(1)} %get-tuple-element.11.refs_0_.refs_6_.v1_ref, f32[16,32,256]{2,1,0:T(8,128)S(1)} %get-tuple-element.15.v2_ref), custom_call_target="tpu_custom_call" | custom-call | tf_op jit(solution)/shard_map/final_update/pallas_call | solution.py:350
  (12 shorter events, 0.2 us)
Async XLA Ops:
  0.6 39.8 %copy-start.3 = (f32[4,4,2,256]{3,2,1,0:T(2,128)S(1)}, f32[4,4,2,256]{3,2,1,0:T(2,128)}, u32[]{:S(2)}) copy-start(f32[4,4,2,256]{3,2,1,0:T(2,128)} %param.4) | copy-start | bytes 98308
  2.5 4.4 %collective-permute-start.1 = (f32[4,34,256]{2,1,0:T(8,128)S(1)}, f32[4,34,256]{2,1,0:T(8,128)S(1)}, u32[]{:S(2)}, u32[]{:S(2)}) collective-permute-start(f32[4,34,256]{2,1,0:T(8,128)S(1)} %get-tuple-element.20), channel_id=1, source_target_pairs={{1,0},{2,1},{3,2},{4,3},{5,4},{6,5},{7,6},{9,8},{10,9},{11,10},{12... | collective-permute-start | bytes 417800 | tf_op jit(solution)/shard_map/ppermute | solution.py:288
  3.8 4.0 %collective-permute-start = (f32[4,34,256]{2,1,0:T(8,128)S(1)}, f32[4,34,256]{2,1,0:T(8,128)S(1)}, u32[]{:S(2)}, u32[]{:S(2)}) collective-permute-start(f32[4,34,256]{2,1,0:T(8,128)S(1)} %get-tuple-element.21), channel_id=1, source_target_pairs={{0,1},{1,2},{2,3},{3,4},{4,5},{5,6},{6,7},{8,9},{9,10},{10,11},{11... | collective-permute-start | bytes 417800 | tf_op jit(solution)/shard_map/ppermute | solution.py:288
  7.9 32.5 %collective-permute-start.2 = (f32[6,34,256]{2,1,0:T(8,128)S(1)}, f32[6,34,256]{2,1,0:T(8,128)S(1)}, u32[]{:S(2)}, u32[]{:S(2)}) collective-permute-start(f32[6,34,256]{2,1,0:T(8,128)S(1)} %pad_maximum_fusion), channel_id=1, source_target_pairs={{0,8},{8,16},{16,24},{1,9},{9,17},{17,25},{2,10},{10,18},{18,26},{... | collective-permute-start | bytes 626696 | tf_op jit(solution)/shard_map/ppermute | solution.py:288
  12.8 27.6 %collective-permute-start.3 = (f32[6,34,256]{2,1,0:T(8,128)S(1)}, f32[6,34,256]{2,1,0:T(8,128)S(1)}, u32[]{:S(2)}, u32[]{:S(2)}) collective-permute-start(f32[6,34,256]{2,1,0:T(8,128)S(1)} %pad_maximum_fusion.1), channel_id=1, source_target_pairs={{8,0},{16,8},{24,16},{9,1},{17,9},{25,17},{10,2},{18,10},{26,18},{... | collective-permute-start | bytes 626696 | tf_op jit(solution)/shard_map/ppermute | solution.py:288
  14.9 1.0 %copy-start = (f32[4,4,32,256]{3,2,1,0:T(8,128)S(1)}, f32[4,4,32,256]{3,2,1,0:T(8,128)}, u32[]{:S(2)}) copy-start(f32[4,4,32,256]{3,2,1,0:T(8,128)} %param.3) | copy-start | bytes 1572868
  16.0 0.8 copy-start.2
  40.4 30.8 %copy-start.1 = (f32[4,4,32,256]{3,2,1,0:T(8,128)S(1)}, f32[4,4,32,256]{3,2,1,0:T(8,128)}, u32[]{:S(2)}) copy-start(f32[4,4,32,256]{3,2,1,0:T(8,128)} %param.3) | copy-start | bytes 1572868
  53.2 4.4 %collective-permute-start.5 = (f32[4,32,256]{2,1,0:T(8,128)S(1)}, f32[4,32,256]{2,1,0:T(8,128)S(1)}, u32[]{:S(2)}, u32[]{:S(2)}) collective-permute-start(f32[4,32,256]{2,1,0:T(8,128)S(1)} %get-tuple-element.24), channel_id=1, source_target_pairs={{1,0},{2,1},{3,2},{4,3},{5,4},{6,5},{7,6},{9,8},{10,9},{11,10},{12... | collective-permute-start | bytes 393224 | tf_op jit(solution)/shard_map/ppermute | solution.py:288
  54.5 4.0 %collective-permute-start.4 = (f32[4,32,256]{2,1,0:T(8,128)S(1)}, f32[4,32,256]{2,1,0:T(8,128)S(1)}, u32[]{:S(2)}, u32[]{:S(2)}) collective-permute-start(f32[4,32,256]{2,1,0:T(8,128)S(1)} %get-tuple-element.25), channel_id=1, source_target_pairs={{0,1},{1,2},{2,3},{3,4},{4,5},{5,6},{6,7},{8,9},{9,10},{10,11},{11... | collective-permute-start | bytes 393224 | tf_op jit(solution)/shard_map/ppermute | solution.py:288
  58.5 12.7 %collective-permute-start.6 = (f32[6,32,256]{2,1,0:T(8,128)S(1)}, f32[6,32,256]{2,1,0:T(8,128)S(1)}, u32[]{:S(2)}, u32[]{:S(2)}) collective-permute-start(f32[6,32,256]{2,1,0:T(8,128)S(1)} %pad_maximum_fusion.2), channel_id=1, source_target_pairs={{0,8},{8,16},{16,24},{1,9},{9,17},{17,25},{2,10},{10,18},{18,26},{... | collective-permute-start | bytes 589832 | tf_op jit(solution)/shard_map/ppermute | solution.py:288
  59.9 11.4 %collective-permute-start.7 = (f32[6,32,256]{2,1,0:T(8,128)S(1)}, f32[6,32,256]{2,1,0:T(8,128)S(1)}, u32[]{:S(2)}, u32[]{:S(2)}) collective-permute-start(f32[6,32,256]{2,1,0:T(8,128)S(1)} %pad_maximum_fusion.3), channel_id=1, source_target_pairs={{8,0},{16,8},{24,16},{9,1},{17,9},{25,17},{10,2},{18,10},{26,18},{... | collective-permute-start | bytes 589832 | tf_op jit(solution)/shard_map/ppermute | solution.py:288
